TPU v7x, 1024 devices: a whole 4x4x32 slice. The times are simulated.
1024 devices in a mesh: dp: 16 (over x_lo, y, core), mp: 32 (over z), pipe: 2 (over x_hi).
Axes of the slice: x: 4 (x_hi: 2, x_lo: 2; x = x_hi * 2 + x_lo), y: 4, z: 32, core: 2. Of those that a mesh axis runs over, the one named last changes fastest.
Arguments:
- activations: bfloat16 [32768, 4096], P(('dp', 'pipe')), may hold values from -6 to 6
- cotangent: bfloat16 [32768, 11008], P(('dp', 'pipe'), 'mp'), may hold values from -0.03125 to 0.03125
- projection_basis: bfloat16 [4096, 1024], P(None, 'mp'), may hold values from -0.09375 to 0.09375
- first_moment: float32 [1024, 11008], P(('dp', 'pipe'), 'mp'), may hold values from -4 to 4
- second_moment: float32 [1024, 11008], P(('dp', 'pipe'), 'mp'), may hold values from 0.25 to 4
Outputs:
- update: float32 [4096, 11008], P(('dp', 'pipe'), 'mp')
- first_new: float32 [1024, 11008], P(('dp', 'pipe'), 'mp')
- second_new: float32 [1024, 11008], P(('dp', 'pipe'), 'mp')
All inputs are finite; a program needn't handle non-finite values.
Results may differ from a plain program's by a relative error of at most 0.0031.
Values may be sent and summed in bfloat16 or wider, within the bound.
No kernel may reach another device: no remote copies, remote signals or barrier semaphores. Data moves between devices by JAX's collectives and lax.ppermute only.
A program may use at most 32 MiB of HBM per device.

v0:
```python
import jax
import jax.numpy as jnp
from jax import lax
from jax.sharding import PartitionSpec as P

beta_first = 0.9
beta_second = 0.999
correction_first = 1.0
correction_second = 0.632304575
epsilon = 1e-08
galore_scale = 0.25


def on_device(activations, cotangent, projection_basis, first_moment, second_moment):
    projected = lax.dot_general(
        projection_basis, activations, (((0,), (1,)), ((), ())), preferred_element_type=jnp.float32
    ).astype(jnp.bfloat16)
    partial_grad = jnp.dot(
        lax.all_gather(projected, "mp", axis=0, tiled=True),
        cotangent,
        preferred_element_type=jnp.float32,
    )
    tile_rows = first_moment.shape[0]
    summed = lax.psum(partial_grad, ("dp", "pipe"))
    grad_tile = lax.dynamic_slice_in_dim(
        summed, lax.axis_index(("dp", "pipe")) * tile_rows, tile_rows, 0
    )
    first_new = beta_first * first_moment + (1.0 - beta_first) * grad_tile
    second_new = beta_second * second_moment + (1.0 - beta_second) * grad_tile * grad_tile
    direction = (
        first_new / correction_first / (jnp.sqrt(second_new / correction_second) + epsilon)
    ).astype(jnp.bfloat16)
    row_block = projection_basis.shape[0] // lax.axis_size(("dp", "pipe"))
    own_rows = lax.dynamic_slice_in_dim(
        projection_basis, lax.axis_index(("dp", "pipe")) * row_block, row_block, 0
    )
    basis_rows = lax.all_gather(own_rows, "mp", axis=1, tiled=True)
    folded = jnp.dot(
        basis_rows,
        lax.all_gather(direction, ("dp", "pipe"), axis=0, tiled=True),
        preferred_element_type=jnp.float32,
    )
    return (galore_scale * folded, first_new, second_new)


def solution(mesh):
    return jax.shard_map(
        on_device,
        mesh=mesh,
        in_specs=(
            P(("dp", "pipe"), None),
            P(("dp", "pipe"), "mp"),
            P(None, "mp"),
            P(("dp", "pipe"), "mp"),
            P(("dp", "pipe"), "mp"),
        ),
        out_specs=(P(("dp", "pipe"), "mp"), P(("dp", "pipe"), "mp"), P(("dp", "pipe"), "mp")),
        check_vma=False,
    )
```

profile of v0, /device:TPU:1, one launch (start us, length us, event | category | flops | bytes accessed | tf_op | source)
XLA Modules:
  0.0 413.7 jit_solution(10354746380303826896)
XLA Ops:
  7.2 0.0 copy-start
  7.2 0.0 all-gather.2.cloned.1.call-start
  7.2 6.8 %convolution_convert_fusion = bf16[32,1024]{1,0:T(8,128)(2,1)} fusion(bf16[4096,32]{0,1:T(8,128)(2,1)} %param.7, bf16[1024,4096]{1,0:T(8,128)(2,1)} %param.5), kind=kOutput, calls=%fused_computation.1 | convolution fusion | flops 268468224 | bytes 8716288 | tf_op jit(solution)/shard_map/dot_general | solution.py:15
  14.0 0.0 all-gather.2.cloned.1.call-update
  14.0 0.0 copy-start.1
  14.0 0.0 copy-start.2
  14.0 0.0 all-reduce.2.cloned.1.call-start
  14.1 126.8 %all-gather.2.cloned.1.call-done = bf16[1024,1024]{1,0:T(8,128)(2,1)} async-done(((bf16[32,1024]{1,0:T(8,128)(2,1)}), bf16[1024,1024]{1,0:T(8,128)(2,1)}) %all-gather.2.cloned.1.call-update) | async-done | bytes 2097168 | tf_op jit(solution)/shard_map/all_gather | solution.py:19
  140.8 0.0 copy-done
  140.8 4.0 fusion.2
  144.8 0.0 all-reduce.2.cloned.1.call-update
  144.9 0.7 constant_dynamic-slice_fusion
  145.6 41.7 %all_gather.9 = bf16[128,1024]{0,1:T(8,128)(2,1)S(1)} all-gather(bf16[128,32]{0,1:T(8,128)(2,1)S(1)} %constant_dynamic-slice_fusion), channel_id=1, replica_groups=mesh['dp'=16,'mp'=32,'pipe'=2] {'mp'}, dimensions={1}, use_global_device_ids=true | all-gather | bytes 270336 | tf_op jit(solution)/shard_map/all_gather | solution.py:37
  187.2 147.4 %all-reduce.2.cloned.1.call-done = f32[1024,344]{1,0:T(8,128)} async-done(((f32[1024,344]{1,0:T(8,128)}), f32[1024,344]{1,0:T(8,128)}) %all-reduce.2.cloned.1.call-update) | async-done | bytes 1409040 | tf_op jit(solution)/shard_map/psum | solution.py:24
  334.6 0.0 copy-done.1
  334.6 0.0 copy-done.2
  334.6 1.5 divide_convert_fusion
  336.1 69.7 %all_gather.11 = bf16[1024,344]{1,0:T(8,128)(2,1)S(1)} all-gather(bf16[32,344]{1,0:T(8,128)(2,1)S(1)} %get-tuple-element.3), channel_id=1, replica_groups=mesh['dp'=16,'mp'=32,'pipe'=2] {'dp','pipe'}, dimensions={0}, use_global_device_ids=true | all-gather | bytes 726528 | tf_op jit(solution)/shard_map/all_gather | solution.py:40
  405.8 1.1 convolution_multiply_fusion
Async XLA Ops:
  7.2 133.7 %copy-start = (bf16[1024,344]{0,1:T(8,128)(2,1)S(1)}, bf16[1024,344]{0,1:T(8,128)(2,1)}, u32[]{:S(2)}) copy-start(bf16[1024,344]{0,1:T(8,128)(2,1)} %param.6) | copy-start | bytes 2113540
  7.2 133.7 %all-gather.2.cloned.1.call-start = ((), (), s32[]{:S(2)}) async-start(), calls=%async_computation | async-start | bytes 2162688 | tf_op jit(solution)/shard_map/all_gather | solution.py:19
  14.0 320.6 %copy-start.1 = (f32[32,344]{1,0:T(8,128)S(1)}, f32[32,344]{1,0:T(8,128)}, u32[]{:S(2)}) copy-start(f32[32,344]{1,0:T(8,128)} %param.9) | copy-start | bytes 132100
  14.0 320.6 %copy-start.2 = (f32[32,344]{1,0:T(8,128)S(1)}, f32[32,344]{1,0:T(8,128)}, u32[]{:S(2)}) copy-start(f32[32,344]{1,0:T(8,128)} %param.8) | copy-start | bytes 132100
  14.0 320.6 %all-reduce.2.cloned.1.call-start = ((), (), s32[]{:S(2)}) async-start(), calls=%async_computation.1 | async-start | bytes 3145728 | tf_op jit(solution)/shard_map/psum | solution.py:24
Sparse Core Ops, SparseCore 0:
  14.1 126.6 all-gather.1
  145.0 189.5 all-reduce.1
where the time goes:
time: 414 us
  waiting for transfers between devices  274 us (66%)
  blocking collectives  111 us (27%)
  between operations  14.1 us (3%)
  matrix products  11.9 us (3%)
    psum x1, waiting for transfers between devices, on_device(): summed = lax.psum(partial_grad, ('dp', 'pipe'))  147 us
    all_gather x1, waiting for transfers between devices, on_device(): lax.all_gather(projected, 'mp', axis=0, tiled=True)  127 us
    all_gather x1, blocking collectives, on_device(): lax.all_gather(direction, ('dp', 'pipe'), axis=0, tiled=True)  69.7 us
    all_gather x1, blocking collectives, on_device(): basis_rows = lax.all_gather(own_rows, 'mp', axis=1, tiled=True)  41.7 us
  transfers between devices with their start and end apart: 2, of which 2 were waited for; matrix products, arithmetic and copies ran while one was open for 0% of the time, Pallas kernels for 0%

commit v1 on v0

v1 whole, which is shorter than its diff:
```python
import jax
import jax.numpy as jnp
from jax import lax
from jax.sharding import PartitionSpec as P

beta_first = 0.9
beta_second = 0.999
correction_first = 1.0
correction_second = 0.632304575
epsilon = 1e-08
galore_scale = 0.25

DATA = ("dp", "pipe")


def spread(x, axes, n):
    return lax.all_to_all(jnp.broadcast_to(x[None], (n, *x.shape)), axes, 0, 0)


def on_device(activations, cotangent, projection_basis, first_moment, second_moment):
    n_data, n_mp = lax.axis_size(DATA), lax.axis_size("mp")
    here = lax.axis_index(DATA)
    width, own_rank = projection_basis.shape
    rows, tile_rows, hidden = width // n_data, first_moment.shape[0], cotangent.shape[1]
    own_rows = lax.dynamic_slice_in_dim(projection_basis, here * rows, rows, 0).T
    basis_rows = spread(own_rows, "mp", n_mp).reshape(n_mp * own_rank, rows)
    whole_grad = lax.dot_general(
        activations, cotangent, (((0,), (0,)), ((), ())), preferred_element_type=jnp.float32
    ).astype(jnp.bfloat16)
    pieces = lax.all_to_all(whole_grad.reshape(n_data, rows, hidden), DATA, 0, 0)
    grad_rows = jnp.sum(pieces.astype(jnp.float32), axis=0)
    high = grad_rows.astype(jnp.bfloat16)
    low = (grad_rows - high.astype(jnp.float32)).astype(jnp.bfloat16)
    partial_grad = (
        jnp.dot(basis_rows, high, preferred_element_type=jnp.float32)
        + jnp.dot(basis_rows, low, preferred_element_type=jnp.float32)
    ).astype(jnp.bfloat16)
    tiles = lax.all_to_all(partial_grad.reshape(n_data, tile_rows, hidden), DATA, 0, 0)
    grad_tile = jnp.sum(tiles.astype(jnp.float32), axis=0)
    first_new = beta_first * first_moment + (1.0 - beta_first) * grad_tile
    second_new = beta_second * second_moment + (1.0 - beta_second) * grad_tile * grad_tile
    direction = (
        first_new / correction_first / (jnp.sqrt(second_new / correction_second) + epsilon)
    ).astype(jnp.bfloat16)
    directions = spread(direction, DATA, n_data).reshape(n_data * tile_rows, hidden)
    folded = lax.dot_general(
        basis_rows, directions, (((0,), (0,)), ((), ())), preferred_element_type=jnp.float32
    )
    return (galore_scale * folded, first_new, second_new)


def solution(mesh):
    return jax.shard_map(
        on_device,
        mesh=mesh,
        in_specs=(
            P(DATA, None),
            P(DATA, "mp"),
            P(None, "mp"),
            P(DATA, "mp"),
            P(DATA, "mp"),
        ),
        out_specs=(P(DATA, "mp"), P(DATA, "mp"), P(DATA, "mp")),
        check_vma=False,
    )
```

time: 414 us -> 171 us (0.41)
  waiting for transfers between devices: 274 us -> 74.9 us
  blocking collectives: 111 us -> 39.7 us
  starting transfers between devices: 0.08 us -> 37 us
  between operations: 14.1 us -> 0.73 us
  local copies, waits for them, and re-layouts: 0.73 us -> 5.03 us
    psum x1 -> x0, waiting for transfers between devices: 147 us -> none  [on_device(): summed = lax.psum(partial_grad, ('dp', 'pipe'))]
    all_gather x1 -> x0, waiting for transfers between devices: 127 us -> none  [on_device(): lax.all_gather(projected, 'mp', axis=0, tiled=True)]
    all_gather x2 -> x0, blocking collectives: 111 us -> none  [the longest x1 69.7 us: on_device(): lax.all_gather(direction, ('dp', 'pipe'), axis=0, tiled=True)]
    all_to_all x0 -> x2, waiting for transfers between devices: none -> 74.9 us  [the longest x1 39.5 us: spread(): return lax.all_to_all(jnp.broadcast_to(x[None], (n, *x.shape)), axes, 0, 0)]
    all_to_all x0 -> x2, blocking collectives: none -> 39.7 us  [the longest x1 21.8 us: on_device(): lax.all_to_all(partial_grad.reshape(n_data, tile_rows, hidden), DATA, 0, 0)]
    all_to_all x0 -> x2, starting transfers between devices: none -> 37 us  [the longest x1 19.1 us: spread(): return lax.all_to_all(jnp.broadcast_to(x[None], (n, *x.shape)), axes, 0, 0)]
    dot_general x3 -> x4, matrix products: 11.9 us -> 11.7 us  [the longest x1 6.79 us: on_device(): lax.dot_general(activations, cotangent, (((0,), (0,)), ((), ())), preferr...]
  transfers between devices with their start and end apart: 2 -> 2, of which waited for: 2 -> 2; matrix products, arithmetic and copies ran while one was open for 0% -> 1% of each run, Pallas kernels for 0% -> 0%
where the time goes in v1:
time: 171 us
  waiting for transfers between devices  74.9 us (44%)
  blocking collectives  39.7 us (23%)
  starting transfers between devices  37 us (22%)
  matrix products  11.7 us (7%)
  local copies, waits for them, and re-layouts  5.03 us (3%)
  other arithmetic  1.86 us (1%)
    all_to_all x1, waiting for transfers between devices, spread(): return lax.all_to_all(jnp.broadcast_to(x[None], (n, *x.shape)), axes, 0, 0)  39.5 us
    all_to_all x1, waiting for transfers between devices, on_device(): lax.all_to_all(whole_grad.reshape(n_data, rows, hidden), DATA, 0, 0)  35.4 us
    all_to_all x1, blocking collectives, on_device(): lax.all_to_all(partial_grad.reshape(n_data, tile_rows, hidden), DATA, 0, 0)  21.8 us
    all_to_all x1, starting transfers between devices, spread(): return lax.all_to_all(jnp.broadcast_to(x[None], (n, *x.shape)), axes, 0, 0)  19.1 us
    all_to_all x1, blocking collectives, spread(): return lax.all_to_all(jnp.broadcast_to(x[None], (n, *x.shape)), axes, 0, 0)  18 us
    all_to_all x1, starting transfers between devices, on_device(): lax.all_to_all(whole_grad.reshape(n_data, rows, hidden), DATA, 0, 0)  17.9 us
    dot_general x1, matrix products, on_device(): lax.dot_general(activations, cotangent, (((0,), (0,)), ((), ())), preferr...  6.79 us
  transfers between devices with their start and end apart: 2, of which 2 were waited for; matrix products, arithmetic and copies ran while one was open for 1% of the time, Pallas kernels for 0%

profile of v1, /device:TPU:1, one launch (start us, length us, event | category | flops | bytes accessed | tf_op | source)
XLA Modules:
  0.0 171.0 jit_solution(16560986769693196942)
XLA Ops:
  0.6 0.0 copy-start
  0.6 1.1 copy-done
  1.7 6.8 %fusion = bf16[43,32,8,128]{3,2,1,0:T(8,128)(2,1)S(1)} fusion(bf16[1024,4096]{1,0:T(8,128)(2,1)} %param.5, bf16[1024,344]{0,1:T(8,128)(2,1)S(1)} %copy-done), kind=kOutput, calls=%fused_computation.3 | convolution fusion | flops 2887090176 | bytes 11911168 | tf_op jit(solution)/shard_map/dot_general | solution.py:27
  8.5 2.0 %copy.15 = bf16[43,32,8,128]{3,2,0,1:T(8,128)(2,1)} copy(bf16[43,32,8,128]{3,2,1,0:T(8,128)(2,1)S(1)} %fusion) | data formatting | bytes 5636096 | tf_op jit(solution)/shard_map/reshape | solution.py:30
  10.6 17.9 %all-to-all-start.1 = ((bf16[32,128,344]{1,2,0:T(8,128)(2,1)}), bf16[32,128,344]{1,2,0:T(8,128)(2,1)S(1)}, u32[]{:S(2)}, u32[]{:S(2)}) async-start(bf16[32,128,344]{1,2,0:T(8,128)(2,1)} %bitcast.19), calls=%async_computation.1 | async-start | bytes 5636096 | tf_op jit(solution)/shard_map/all_to_all | solution.py:30
  28.5 0.7 dynamic-slice_bitcast_fusion
  29.2 35.4 %all-to-all-done.1 = bf16[32,128,344]{1,2,0:T(8,128)(2,1)S(1)} async-done(((bf16[32,128,344]{1,2,0:T(8,128)(2,1)}), bf16[32,128,344]{1,2,0:T(8,128)(2,1)S(1)}, u32[]{:S(2)}, u32[]{:S(2)}) %all-to-all-start.1) | async-done | bytes 2818080 | tf_op jit(solution)/shard_map/all_to_all | solution.py:30
  64.6 0.7 broadcast_in_dim.4
  65.3 19.1 %all-to-all-start = ((bf16[32,32,128]{2,1,0:T(8,128)(2,1)}), bf16[32,32,128]{2,1,0:T(8,128)(2,1)}, u32[]{:S(2)}, u32[]{:S(2)}) async-start(bf16[32,32,128]{2,1,0:T(8,128)(2,1)} %broadcast_in_dim.4), calls=%async_computation | async-start | bytes 524288 | tf_op jit(solution)/shard_map/all_to_all | solution.py:17
  84.5 1.1 convert_reduce_fusion
  85.6 39.5 %all-to-all-done = bf16[32,32,128]{2,1,0:T(8,128)(2,1)} async-done(((bf16[32,32,128]{2,1,0:T(8,128)(2,1)}), bf16[32,32,128]{2,1,0:T(8,128)(2,1)}, u32[]{:S(2)}, u32[]{:S(2)}) %all-to-all-start) | async-done | bytes 262176 | tf_op jit(solution)/shard_map/all_to_all | solution.py:17
  125.0 1.4 fusion.5
  126.4 0.0 copy-start.1
  126.4 0.0 copy-start.2
  126.4 1.5 fusion.1
  127.9 0.4 copy.11
  128.3 21.8 %all_to_all.20 = bf16[32,32,344]{2,1,0:T(8,128)(2,1)S(1)} all-to-all(bf16[32,32,344]{2,1,0:T(8,128)(2,1)S(1)} %bitcast.20), channel_id=1, replica_groups=mesh['dp'=16,'mp'=32,'pipe'=2] {'dp','pipe'}, dimensions={0} | all-to-all | bytes 1409024 | tf_op jit(solution)/shard_map/all_to_all | solution.py:38
  150.0 0.1 convert_reduce_fusion.1
  150.2 0.0 copy-done.1
  150.2 0.0 copy-done.2
  150.2 0.7 divide_convert_fusion
  150.8 0.1 broadcast_in_dim.5
  150.9 18.0 %all_to_all.21 = bf16[32,32,344]{2,1,0:T(8,128)(2,1)S(1)} all-to-all(bf16[32,32,344]{2,1,0:T(8,128)(2,1)S(1)} %broadcast_in_dim.5), channel_id=1, replica_groups=mesh['dp'=16,'mp'=32,'pipe'=2] {'dp','pipe'}, dimensions={0} | all-to-all | bytes 1409024 | tf_op jit(solution)/shard_map/all_to_all | solution.py:17
  168.9 2.1 %fusion.2 = f32[128,344]{0,1:T(8,128)} fusion(bf16[32,32,128]{2,1,0:T(8,128)(2,1)} %all-to-all-done, bf16[32,32,344]{2,1,0:T(8,128)(2,1)S(1)} %all_to_all.21), kind=kOutput, calls=%fused_computation.8 | convolution fusion | flops 90221568 | bytes 1142784 | tf_op jit(solution)/shard_map/dot_general | solution.py:46
Async XLA Ops:
  0.6 1.1 copy-start
  10.6 54.0 %all-to-all-start.1 = ((bf16[32,128,344]{1,2,0:T(8,128)(2,1)}), bf16[32,128,344]{1,2,0:T(8,128)(2,1)S(1)}, u32[]{:S(2)}, u32[]{:S(2)}) async-start(bf16[32,128,344]{1,2,0:T(8,128)(2,1)} %bitcast.19), calls=%async_computation.1 | async-start | bytes 5636096 | tf_op jit(solution)/shard_map/all_to_all | solution.py:30
  65.3 59.7 %all-to-all-start = ((bf16[32,32,128]{2,1,0:T(8,128)(2,1)}), bf16[32,32,128]{2,1,0:T(8,128)(2,1)}, u32[]{:S(2)}, u32[]{:S(2)}) async-start(bf16[32,32,128]{2,1,0:T(8,128)(2,1)} %broadcast_in_dim.4), calls=%async_computation | async-start | bytes 524288 | tf_op jit(solution)/shard_map/all_to_all | solution.py:17
  126.4 23.8 %copy-start.1 = (f32[32,344]{1,0:T(8,128)S(1)}, f32[32,344]{1,0:T(8,128)}, u32[]{:S(2)}) copy-start(f32[32,344]{1,0:T(8,128)} %param.9) | copy-start | bytes 132100
  126.4 23.8 %copy-start.2 = (f32[32,344]{1,0:T(8,128)S(1)}, f32[32,344]{1,0:T(8,128)}, u32[]{:S(2)}) copy-start(f32[32,344]{1,0:T(8,128)} %param.8) | copy-start | bytes 132100

commit v2 on v1

v2 whole, which is shorter than its diff:
```python
import jax
import jax.numpy as jnp
from jax import lax
from jax.experimental import pallas as pl
from jax.experimental.pallas import tpu as pltpu
from jax.sharding import Mesh, PartitionSpec as P

beta_first = 0.9
beta_second = 0.999
correction_first = 1.0
correction_second = 0.632304575
epsilon = 1e-08
galore_scale = 0.25

DATA = ("xl", "y", "core", "xh")
MP = ("far", "near")


def spread(x, axes):
    n = lax.axis_size(axes)
    return lax.all_to_all(jnp.broadcast_to(x[None], (n, *x.shape)), axes, 0, 0)


def grad_kernel(cot_ref, act_ref, out_ref):
    block = jnp.dot(cot_ref[...], act_ref[...], preferred_element_type=jnp.float32)
    width = out_ref.shape[2]
    for piece in range(out_ref.shape[0]):
        out_ref[piece] = block[:, piece * width : (piece + 1) * width].astype(out_ref.dtype)


def whole_grad(cotangent, activations, pieces, per_step=2):
    tokens, width = activations.shape
    hidden = cotangent.shape[0]
    cols = width // pieces
    return pl.pallas_call(
        grad_kernel,
        grid=(pieces // per_step,),
        in_specs=[
            pl.BlockSpec((hidden, tokens), lambda i: (0, 0)),
            pl.BlockSpec((tokens, per_step * cols), lambda i: (0, i)),
        ],
        out_specs=pl.BlockSpec((per_step, hidden, cols), lambda i: (i, 0, 0)),
        out_shape=jax.ShapeDtypeStruct((pieces, hidden, cols), jnp.bfloat16),
        compiler_params=pltpu.CompilerParams(vmem_limit_bytes=32 << 20),
        name="whole_grad",
    )(cotangent, activations)


def on_device(activations, cotangent, projection_basis, first_moment, second_moment):
    n_data = lax.axis_size(DATA)
    here = lax.axis_index(DATA)
    width, own_rank = projection_basis.shape
    rows, tile_rows, hidden = width // n_data, first_moment.shape[0], cotangent.shape[1]

    own_rows = lax.dynamic_slice_in_dim(projection_basis.T, here * rows, rows, 1)
    near_rows = spread(own_rows, "near")
    pieces = whole_grad(cotangent.T, activations, n_data)
    pieces, near_rows = lax.optimization_barrier((pieces, near_rows))
    basis_rows = lax.all_gather(near_rows, "far", axis=0).reshape(-1, rows)

    pieces = lax.all_to_all(pieces, DATA, 0, 0)
    grad_rows = jnp.sum(pieces.astype(jnp.float32), axis=0)
    high = grad_rows.astype(jnp.bfloat16)
    low = (grad_rows - high.astype(jnp.float32)).astype(jnp.bfloat16)
    partial_grad = jnp.dot(
        jnp.concatenate([basis_rows, basis_rows], axis=1),
        jnp.concatenate([high, low], axis=1).T,
        preferred_element_type=jnp.float32,
    ).astype(jnp.bfloat16)
    tiles = lax.all_to_all(partial_grad.reshape(n_data, tile_rows, hidden), DATA, 0, 0)
    grad_tile = jnp.sum(tiles.astype(jnp.float32), axis=0)
    first_new = beta_first * first_moment + (1.0 - beta_first) * grad_tile
    second_new = beta_second * second_moment + (1.0 - beta_second) * grad_tile * grad_tile
    direction = (
        first_new / correction_first / (jnp.sqrt(second_new / correction_second) + epsilon)
    ).astype(jnp.bfloat16)
    directions = spread(direction, DATA).reshape(n_data * tile_rows, hidden)
    folded = lax.dot_general(
        basis_rows, directions, (((0,), (0,)), ((), ())), preferred_element_type=jnp.float32
    )
    return (galore_scale * folded, first_new, second_new)


def solution(mesh):
    dp, mp, pipe = mesh.devices.shape
    fine = Mesh(
        mesh.devices.reshape(2, dp // 4, 2, 4, mp // 4, pipe),
        ("xl", "y", "core", "far", "near", "xh"),
    )
    return jax.shard_map(
        on_device,
        mesh=fine,
        in_specs=(
            P(DATA, None),
            P(DATA, MP),
            P(None, MP),
            P(DATA, MP),
            P(DATA, MP),
        ),
        out_specs=(P(DATA, MP), P(DATA, MP), P(DATA, MP)),
        check_vma=False,
    )
```

time: 171 us -> 124 us (0.73)
  waiting for transfers between devices: 74.9 us -> 0.01 us
  blocking collectives: 39.7 us -> 82.7 us
  starting transfers between devices: 37 us -> 21.2 us
  matrix products: 11.7 us -> 1.49 us
  Pallas kernels: 0 us -> 9.33 us
    all_to_all x1, waiting for transfers between devices: 39.5 us -> 0.01 us  [spread(): return lax.all_to_all(jnp.broadcast_to(x[None], (n, *x.shape)), axes, 0, 0)]
    all_gather x0 -> x1, blocking collectives: none -> 39.3 us  [on_device(): basis_rows = lax.all_gather(near_rows, 'far', axis=0).reshape(-1, rows)]
    all_to_all x1, waiting for transfers between devices: 35.4 us -> 0.01 us  [on_device(): pieces = lax.all_to_all(pieces, DATA, 0, 0)]
    all_to_all x1, starting transfers between devices: 17.9 us -> 8.16 us  [on_device(): pieces = lax.all_to_all(pieces, DATA, 0, 0)]
    pallas_call x0 -> x1, Pallas kernels: none -> 9.33 us  [whole_grad(): pl.pallas_call(grad_kernel, grid=(pieces // per_step,), in_specs=[pl.Bloc...]
    dot_general x3 -> x1, matrix products: 9.63 us -> 0.38 us  [on_device(): jnp.dot(jnp.concatenate([basis_rows, basis_rows], axis=1), jnp.concatenat...]
    all_to_all x1, starting transfers between devices: 19.1 us -> 13.1 us  [spread(): return lax.all_to_all(jnp.broadcast_to(x[None], (n, *x.shape)), axes, 0, 0)]
    unnamed x6 -> x10, local copies, waits for them, and re-layouts: 1.12 us -> 5.43 us
  transfers between devices with their start and end apart: 2 -> 2, of which waited for: 2 -> 0; matrix products, arithmetic and copies ran while one was open for 1% -> 0% of each run, Pallas kernels for 0% -> 8%
where the time goes in v2:
time: 124 us; the launch traced here: 123 us
  blocking collectives  82.7 us (67%)
  starting transfers between devices  21.2 us (17%)
  Pallas kernels  9.33 us (8%)
  local copies, waits for them, and re-layouts  6.5 us (5%)
  matrix products  1.49 us (1%)
    all_gather x1, blocking collectives, on_device(): basis_rows = lax.all_gather(near_rows, 'far', axis=0).reshape(-1, rows)  39.3 us
    all_to_all x1, blocking collectives, on_device(): lax.all_to_all(partial_grad.reshape(n_data, tile_rows, hidden), DATA, 0, 0)  25.4 us
    all_to_all x1, blocking collectives, spread(): return lax.all_to_all(jnp.broadcast_to(x[None], (n, *x.shape)), axes, 0, 0)  18 us
    all_to_all x1, starting transfers between devices, spread(): return lax.all_to_all(jnp.broadcast_to(x[None], (n, *x.shape)), axes, 0, 0)  13.1 us
    pallas_call x1, Pallas kernels, whole_grad(): pl.pallas_call(grad_kernel, grid=(pieces // per_step,), in_specs=[pl.Bloc...  9.33 us
    all_to_all x1, starting transfers between devices, on_device(): pieces = lax.all_to_all(pieces, DATA, 0, 0)  8.16 us
    unnamed x10, local copies, waits for them, and re-layouts  5.43 us
  transfers between devices with their start and end apart: 2, of which 0 were waited for; matrix products, arithmetic and copies ran while one was open for 0% of the time, Pallas kernels for 8%

profile of v2, /device:TPU:1, one launch (start us, length us, event | category | flops | bytes accessed | tf_op | source)
XLA Modules:
  0.0 123.2 jit_solution(1936630069109116260)
XLA Ops:
  0.6 0.0 copy-start
  0.7 0.9 copy-done
  1.6 0.6 broadcast_in_dim.4
  2.2 13.1 %all-to-all-start = ((bf16[8,32,128]{2,1,0:T(8,128)(2,1)}), bf16[8,32,128]{2,1,0:T(8,128)(2,1)S(1)}, u32[]{:S(2)}, u32[]{:S(2)}) async-start(bf16[8,32,128]{2,1,0:T(8,128)(2,1)} %broadcast_in_dim.4), calls=%async_computation | async-start | bytes 131072 | tf_op jit(solution)/shard_map/all_to_all | solution.py:21
  15.3 0.0 copy-start.1
  15.3 3.4 %copy-done.1 = bf16[1024,4096]{1,0:T(8,128)(2,1)S(1)} copy-done((bf16[1024,4096]{1,0:T(8,128)(2,1)S(1)}, bf16[1024,4096]{1,0:T(8,128)(2,1)}, u32[]{:S(2)}) %copy-start.1) | copy-done | bytes 8388632
  18.7 0.0 copy-start.2
  18.7 1.1 copy-done.2
  19.8 9.3 %whole_grad.1 = bf16[32,344,128]{2,1,0:T(8,128)(2,1)} custom-call(bf16[344,1024]{1,0:T(8,128)(2,1)S(1)} %bitcast.8, bf16[1024,4096]{1,0:T(8,128)(2,1)S(1)} %copy-done.1), custom_call_target="tpu_custom_call" | custom-call | tf_op jit(solution)/shard_map/whole_grad/pallas_call | solution.py:35
  29.1 0.0 all-to-all-done
  29.1 8.2 %all-to-all-start.1 = ((bf16[32,344,128]{2,1,0:T(8,128)(2,1)}), bf16[32,344,128]{2,1,0:T(8,128)(2,1)S(1)}, u32[]{:S(2)}, u32[]{:S(2)}) async-start(bf16[32,344,128]{2,1,0:T(8,128)(2,1)} %whole_grad.1), calls=%async_computation.1 | async-start | bytes 5636096 | tf_op jit(solution)/shard_map/all_to_all | solution.py:61
  37.3 39.3 %all-gather = bf16[32,32,128]{2,1,0:T(8,128)(2,1)S(1)} all-gather(bf16[8,32,128]{2,1,0:T(8,128)(2,1)S(1)} %all-to-all-done), channel_id=2, replica_groups=mesh['xl'=2,'y'=4,'core'=2,'far'=4,'near'=8,'xh'=2] {'far'}, dimensions={0}, use_global_device_ids=true | all-gather | bytes 327680 | tf_op jit(solution)/shard_map/all_gather | solution.py:59
  76.6 0.0 all-to-all-done.1
  76.6 0.4 convert_reduce_fusion
  77.1 0.0 copy-start.3
  77.1 0.0 copy-start.4
  77.1 0.4 convolution_convert_fusion
  77.5 0.4 copy.9
  77.8 25.4 %all_to_all.20 = bf16[32,32,344]{2,1,0:T(8,128)(2,1)S(1)} all-to-all(bf16[32,32,344]{2,1,0:T(8,128)(2,1)S(1)} %bitcast.10), channel_id=1, replica_groups=mesh['xl'=2,'y'=4,'core'=2,'far'=4,'near'=8,'xh'=2] {'xl','y','core','xh'}, dimensions={0} | all-to-all | bytes 1409024 | tf_op jit(solution)/shard_map/all_to_all | solution.py:70
  103.2 0.1 convert_reduce_fusion.1
  103.3 0.0 copy-done.3
  103.4 0.0 copy-done.4
  103.4 0.7 divide_convert_fusion
  104.0 0.1 broadcast_in_dim.5
  104.1 18.0 %all_to_all.21 = bf16[32,32,344]{2,1,0:T(8,128)(2,1)S(1)} all-to-all(bf16[32,32,344]{2,1,0:T(8,128)(2,1)S(1)} %broadcast_in_dim.5), channel_id=1, replica_groups=mesh['xl'=2,'y'=4,'core'=2,'far'=4,'near'=8,'xh'=2] {'xl','y','core','xh'}, dimensions={0} | all-to-all | bytes 1409024 | tf_op jit(solution)/shard_map/all_to_all | solution.py:21
  122.1 1.1 convolution_multiply_fusion
  (2 shorter events, 0.0 us)
Async XLA Ops:
  0.6 1.0 copy-start
  2.2 26.9 %all-to-all-start = ((bf16[8,32,128]{2,1,0:T(8,128)(2,1)}), bf16[8,32,128]{2,1,0:T(8,128)(2,1)S(1)}, u32[]{:S(2)}, u32[]{:S(2)}) async-start(bf16[8,32,128]{2,1,0:T(8,128)(2,1)} %broadcast_in_dim.4), calls=%async_computation | async-start | bytes 131072 | tf_op jit(solution)/shard_map/all_to_all | solution.py:21
  15.3 3.4 %copy-start.1 = (bf16[1024,4096]{1,0:T(8,128)(2,1)S(1)}, bf16[1024,4096]{1,0:T(8,128)(2,1)}, u32[]{:S(2)}) copy-start(bf16[1024,4096]{1,0:T(8,128)(2,1)} %act_ref.1) | copy-start | bytes 25165828
  18.7 1.1 copy-start.2
  29.1 47.5 %all-to-all-start.1 = ((bf16[32,344,128]{2,1,0:T(8,128)(2,1)}), bf16[32,344,128]{2,1,0:T(8,128)(2,1)S(1)}, u32[]{:S(2)}, u32[]{:S(2)}) async-start(bf16[32,344,128]{2,1,0:T(8,128)(2,1)} %whole_grad.1), calls=%async_computation.1 | async-start | bytes 5636096 | tf_op jit(solution)/shard_map/all_to_all | solution.py:61
  77.1 26.3 %copy-start.3 = (f32[32,344]{1,0:T(8,128)S(1)}, f32[32,344]{1,0:T(8,128)}, u32[]{:S(2)}) copy-start(f32[32,344]{1,0:T(8,128)} %param.9) | copy-start | bytes 132100
  77.1 26.3 %copy-start.4 = (f32[32,344]{1,0:T(8,128)S(1)}, f32[32,344]{1,0:T(8,128)}, u32[]{:S(2)}) copy-start(f32[32,344]{1,0:T(8,128)} %param.8) | copy-start | bytes 132100

commit v3 on v2

--- a/solution.py
+++ b/solution.py
@@ -21,29 +21,61 @@
     return lax.all_to_all(jnp.broadcast_to(x[None], (n, *x.shape)), axes, 0, 0)
 
 
-def grad_kernel(cot_ref, act_ref, out_ref):
-    block = jnp.dot(cot_ref[...], act_ref[...], preferred_element_type=jnp.float32)
-    width = out_ref.shape[2]
-    for piece in range(out_ref.shape[0]):
-        out_ref[piece] = block[:, piece * width : (piece + 1) * width].astype(out_ref.dtype)
+def grad_kernel(cot_hbm, act_hbm, out_hbm, cot, act, out, cot_sem, in_sem, out_sem):
+    chunks, per_chunk, width = out.shape[0], out.shape[1], out.shape[3]
+    cols = per_chunk * width
+
+    def fetch(c):
+        return pltpu.make_async_copy(
+            act_hbm.at[:, c * cols : (c + 1) * cols], act.at[c], in_sem.at[c]
+        )
+
+    def send(c):
+        return pltpu.make_async_copy(
+            out.at[c], out_hbm.at[c * per_chunk : (c + 1) * per_chunk], out_sem.at[c]
+        )
+
+    whole = pltpu.make_async_copy(cot_hbm, cot, cot_sem)
+    whole.start()
+    for c in range(chunks):
+        fetch(c).start()
+    whole.wait()
+    for c in range(chunks):
+        fetch(c).wait()
+        block = jnp.dot(cot[...], act[c], preferred_element_type=jnp.float32)
+        for p in range(per_chunk):
+            out[c, p] = block[:, p * width : (p + 1) * width].astype(out.dtype)
+        send(c).start()
+    for c in range(chunks):
+        send(c).wait()
 
 
-def whole_grad(cotangent, activations, pieces, per_step=2):
+def whole_grad(cotangent, activations, pieces, chunks=2):
     tokens, width = activations.shape
-    hidden = cotangent.shape[0]
-    cols = width // pieces
+    hidden, cols = cotangent.shape[0], width // pieces
+    per_chunk = pieces // chunks
     return pl.pallas_call(
         grad_kernel,
-        grid=(pieces // per_step,),
         in_specs=[
-            pl.BlockSpec((hidden, tokens), lambda i: (0, 0)),
-            pl.BlockSpec((tokens, per_step * cols), lambda i: (0, i)),
+            pl.BlockSpec(memory_space=pltpu.HBM),
+            pl.BlockSpec(memory_space=pltpu.HBM),
         ],
-        out_specs=pl.BlockSpec((per_step, hidden, cols), lambda i: (i, 0, 0)),
+        out_specs=pl.BlockSpec(memory_space=pltpu.HBM),
         out_shape=jax.ShapeDtypeStruct((pieces, hidden, cols), jnp.bfloat16),
-        compiler_params=pltpu.CompilerParams(vmem_limit_bytes=32 << 20),
+        scratch_shapes=[
+            pltpu.VMEM(cotangent.shape, cotangent.dtype),
+            pltpu.VMEM((chunks, tokens, per_chunk * cols), jnp.bfloat16),
+            pltpu.VMEM((chunks, per_chunk, hidden, cols), jnp.bfloat16),
+            pltpu.SemaphoreType.DMA,
+            pltpu.SemaphoreType.DMA((chunks,)),
+            pltpu.SemaphoreType.DMA((chunks,)),
+        ],
+        compiler_params=pltpu.CompilerParams(vmem_limit_bytes=40 << 20),
         name="whole_grad",
-    )(cotangent, activations)
+    )(
+        pltpu.with_memory_space_constraint(cotangent, pltpu.HBM),
+        pltpu.with_memory_space_constraint(activations, pltpu.HBM),
+    )
 
 
 def on_device(activations, cotangent, projection_basis, first_moment, second_moment):

time: 124 us -> 121 us (0.976)
  local copies, waits for them, and re-layouts: 6.5 us -> 2.02 us
  waiting for transfers between devices: 0.01 us -> 2.93 us
  Pallas kernels: 9.33 us -> 6.82 us
    unnamed x10 -> x6, local copies, waits for them, and re-layouts: 5.43 us -> 0.95 us
    all_to_all x1, waiting for transfers between devices: 0.01 us -> 2.92 us  [spread(): return lax.all_to_all(jnp.broadcast_to(x[None], (n, *x.shape)), axes, 0, 0)]
    pallas_call x1, Pallas kernels: 9.33 us -> 6.82 us  [whole_grad(): pl.pallas_call(grad_kernel, in_specs=[pl.BlockSpec(memory_space=pltpu.HBM...]
    all_gather x1, blocking collectives: 39.3 us -> 40.8 us  [on_device(): basis_rows = lax.all_gather(near_rows, 'far', axis=0).reshape(-1, rows)]
    all_to_all x1, blocking collectives: 25.4 us -> 23.9 us  [on_device(): lax.all_to_all(partial_grad.reshape(n_data, tile_rows, hidden), DATA, 0, 0)]
  transfers between devices with their start and end apart: 2 -> 2, of which waited for: 0 -> 1; matrix products, arithmetic and copies ran while one was open for 0% -> 0% of each run, Pallas kernels for 8% -> 6%
where the time goes in v3:
time: 121 us; the launch traced here: 120 us
  blocking collectives  82.7 us (68%)
  starting transfers between devices  22.3 us (18%)
  Pallas kernels  6.82 us (6%)
  waiting for transfers between devices  2.93 us (2%)
  local copies, waits for them, and re-layouts  2.02 us (2%)
  matrix products  1.49 us (1%)
  other arithmetic  1.22 us (1%)
    all_gather x1, blocking collectives, on_device(): basis_rows = lax.all_gather(near_rows, 'far', axis=0).reshape(-1, rows)  40.8 us
    all_to_all x1, blocking collectives, on_device(): lax.all_to_all(partial_grad.reshape(n_data, tile_rows, hidden), DATA, 0, 0)  23.9 us
    all_to_all x1, blocking collectives, spread(): return lax.all_to_all(jnp.broadcast_to(x[None], (n, *x.shape)), axes, 0, 0)  18 us
    all_to_all x1, starting transfers between devices, spread(): return lax.all_to_all(jnp.broadcast_to(x[None], (n, *x.shape)), axes, 0, 0)  13.1 us
    all_to_all x1, starting transfers between devices, on_device(): pieces = lax.all_to_all(pieces, DATA, 0, 0)  9.25 us
    pallas_call x1, Pallas kernels, whole_grad(): pl.pallas_call(grad_kernel, in_specs=[pl.BlockSpec(memory_space=pltpu.HBM...  6.82 us
    all_to_all x1, waiting for transfers between devices, spread(): return lax.all_to_all(jnp.broadcast_to(x[None], (n, *x.shape)), axes, 0, 0)  2.92 us
  transfers between devices with their start and end apart: 2, of which 1 were waited for; matrix products, arithmetic and copies ran while one was open for 0% of the time, Pallas kernels for 6%

profile of v3, /device:TPU:1, one launch (start us, length us, event | category | flops | bytes accessed | tf_op | source)
XLA Modules:
  0.0 120.2 jit_solution(16226027945594850679)
XLA Ops:
  0.6 0.0 copy-start
  0.7 0.9 copy-done
  1.6 0.6 broadcast_in_dim.4
  2.2 13.1 %all-to-all-start = ((bf16[8,32,128]{2,1,0:T(8,128)(2,1)}), bf16[8,32,128]{2,1,0:T(8,128)(2,1)S(1)}, u32[]{:S(2)}, u32[]{:S(2)}) async-start(bf16[8,32,128]{2,1,0:T(8,128)(2,1)} %broadcast_in_dim.4), calls=%async_computation | async-start | bytes 131072 | tf_op jit(solution)/shard_map/all_to_all | solution.py:21
  15.3 6.8 %whole_grad.1 = bf16[32,344,128]{2,1,0:T(8,128)(2,1)} custom-call(bf16[344,1024]{1,0:T(8,128)(2,1)} %bitcast.12, bf16[1024,4096]{1,0:T(8,128)(2,1)} %act_hbm.1), custom_call_target="tpu_custom_call" | custom-call | tf_op jit(solution)/shard_map/whole_grad/pallas_call | solution.py:57
  22.1 2.9 %all-to-all-done = bf16[8,32,128]{2,1,0:T(8,128)(2,1)S(1)} async-done(((bf16[8,32,128]{2,1,0:T(8,128)(2,1)}), bf16[8,32,128]{2,1,0:T(8,128)(2,1)S(1)}, u32[]{:S(2)}, u32[]{:S(2)}) %all-to-all-start) | async-done | bytes 65568 | tf_op jit(solution)/shard_map/all_to_all | solution.py:21
  25.1 9.2 %all-to-all-start.1 = ((bf16[32,344,128]{2,1,0:T(8,128)(2,1)}), bf16[32,344,128]{2,1,0:T(8,128)(2,1)S(1)}, u32[]{:S(2)}, u32[]{:S(2)}) async-start(bf16[32,344,128]{2,1,0:T(8,128)(2,1)} %whole_grad.1), calls=%async_computation.1 | async-start | bytes 5636096 | tf_op jit(solution)/shard_map/all_to_all | solution.py:93
  34.3 40.8 %all-gather = bf16[32,32,128]{2,1,0:T(8,128)(2,1)S(1)} all-gather(bf16[8,32,128]{2,1,0:T(8,128)(2,1)S(1)} %all-to-all-done), channel_id=2, replica_groups=mesh['xl'=2,'y'=4,'core'=2,'far'=4,'near'=8,'xh'=2] {'far'}, dimensions={0}, use_global_device_ids=true | all-gather | bytes 327680 | tf_op jit(solution)/shard_map/all_gather | solution.py:91
  75.1 0.0 all-to-all-done.1
  75.1 0.4 convert_reduce_fusion
  75.6 0.0 copy-start.1
  75.6 0.0 copy-start.2
  75.6 0.4 convolution_convert_fusion
  76.0 0.4 copy.9
  76.3 23.9 %all_to_all.20 = bf16[32,32,344]{2,1,0:T(8,128)(2,1)S(1)} all-to-all(bf16[32,32,344]{2,1,0:T(8,128)(2,1)S(1)} %bitcast.9), channel_id=1, replica_groups=mesh['xl'=2,'y'=4,'core'=2,'far'=4,'near'=8,'xh'=2] {'xl','y','core','xh'}, dimensions={0} | all-to-all | bytes 1409024 | tf_op jit(solution)/shard_map/all_to_all | solution.py:102
  100.2 0.1 convert_reduce_fusion.1
  100.4 0.0 copy-done.1
  100.4 0.0 copy-done.2
  100.4 0.7 divide_convert_fusion
  101.0 0.1 broadcast_in_dim.5
  101.1 18.0 %all_to_all.21 = bf16[32,32,344]{2,1,0:T(8,128)(2,1)S(1)} all-to-all(bf16[32,32,344]{2,1,0:T(8,128)(2,1)S(1)} %broadcast_in_dim.5), channel_id=1, replica_groups=mesh['xl'=2,'y'=4,'core'=2,'far'=4,'near'=8,'xh'=2] {'xl','y','core','xh'}, dimensions={0} | all-to-all | bytes 1409024 | tf_op jit(solution)/shard_map/all_to_all | solution.py:21
  119.1 1.1 convolution_multiply_fusion
  (2 shorter events, 0.0 us)
Async XLA Ops:
  0.6 1.0 copy-start
  2.2 22.8 %all-to-all-start = ((bf16[8,32,128]{2,1,0:T(8,128)(2,1)}), bf16[8,32,128]{2,1,0:T(8,128)(2,1)S(1)}, u32[]{:S(2)}, u32[]{:S(2)}) async-start(bf16[8,32,128]{2,1,0:T(8,128)(2,1)} %broadcast_in_dim.4), calls=%async_computation | async-start | bytes 131072 | tf_op jit(solution)/shard_map/all_to_all | solution.py:21
  25.1 50.1 %all-to-all-start.1 = ((bf16[32,344,128]{2,1,0:T(8,128)(2,1)}), bf16[32,344,128]{2,1,0:T(8,128)(2,1)S(1)}, u32[]{:S(2)}, u32[]{:S(2)}) async-start(bf16[32,344,128]{2,1,0:T(8,128)(2,1)} %whole_grad.1), calls=%async_computation.1 | async-start | bytes 5636096 | tf_op jit(solution)/shard_map/all_to_all | solution.py:93
  75.6 24.8 %copy-start.1 = (f32[32,344]{1,0:T(8,128)S(1)}, f32[32,344]{1,0:T(8,128)}, u32[]{:S(2)}) copy-start(f32[32,344]{1,0:T(8,128)} %param.9) | copy-start | bytes 132100
  75.6 24.8 %copy-start.2 = (f32[32,344]{1,0:T(8,128)S(1)}, f32[32,344]{1,0:T(8,128)}, u32[]{:S(2)}) copy-start(f32[32,344]{1,0:T(8,128)} %param.8) | copy-start | bytes 132100

commit v4 on v3

--- a/solution.py
+++ b/solution.py
@@ -13,6 +13,7 @@
 galore_scale = 0.25
 
 DATA = ("xl", "y", "core", "xh")
+CHIPS = ("xl", "y", "xh")
 MP = ("far", "near")
 
 
@@ -106,7 +107,9 @@
     direction = (
         first_new / correction_first / (jnp.sqrt(second_new / correction_second) + epsilon)
     ).astype(jnp.bfloat16)
-    directions = spread(direction, DATA).reshape(n_data * tile_rows, hidden)
+    directions = lax.all_gather(spread(direction, CHIPS), "core", axis=0)
+    directions = directions.reshape(2, -1, 2, tile_rows, hidden).transpose(1, 0, 2, 3, 4)
+    directions = directions.reshape(n_data * tile_rows, hidden)
     folded = lax.dot_general(
         basis_rows, directions, (((0,), (0,)), ((), ())), preferred_element_type=jnp.float32
     )
@@ -116,7 +119,7 @@
 def solution(mesh):
     dp, mp, pipe = mesh.devices.shape
     fine = Mesh(
-        mesh.devices.reshape(2, dp // 4, 2, 4, mp // 4, pipe),
+        mesh.devices.reshape(2, dp // 4, 2, mp // 4, 4, pipe),
         ("xl", "y", "core", "far", "near", "xh"),
     )
     return jax.shard_map(

time: 121 us -> 115 us (0.950)
  waiting for transfers between devices: 2.93 us -> 0.01 us
  blocking collectives: 82.7 us -> 81.1 us
    all_to_all x1, blocking collectives: 18 us -> 11.1 us  [spread(): return lax.all_to_all(jnp.broadcast_to(x[None], (n, *x.shape)), axes, 0, 0)]
    all_to_all x1, starting transfers between devices: 13.1 us -> 6.44 us  [spread(): return lax.all_to_all(jnp.broadcast_to(x[None], (n, *x.shape)), axes, 0, 0)]
    all_to_all x1, starting transfers between devices: 9.25 us -> 14.7 us  [on_device(): pieces = lax.all_to_all(pieces, DATA, 0, 0)]
    all_gather x0 -> x1, blocking collectives: none -> 4.42 us  [on_device(): directions = lax.all_gather(spread(direction, CHIPS), 'core', axis=0)]
    all_to_all x1, waiting for transfers between devices: 2.92 us -> 0.01 us  [spread(): return lax.all_to_all(jnp.broadcast_to(x[None], (n, *x.shape)), axes, 0, 0)]
    all_to_all x1, blocking collectives: 23.9 us -> 26.6 us  [on_device(): lax.all_to_all(partial_grad.reshape(n_data, tile_rows, hidden), DATA, 0, 0)]
    all_gather x1, blocking collectives: 40.8 us -> 39 us  [on_device(): basis_rows = lax.all_gather(near_rows, 'far', axis=0).reshape(-1, rows)]
  transfers between devices with their start and end apart: 2 -> 2, of which waited for: 1 -> 0; matrix products, arithmetic and copies ran while one was open for 0% -> 0% of each run, Pallas kernels for 6% -> 6%
where the time goes in v4:
time: 115 us
  blocking collectives  81.1 us (71%)
  starting transfers between devices  21.2 us (18%)
  Pallas kernels  6.82 us (6%)
  local copies, waits for them, and re-layouts  2.05 us (2%)
  matrix products  1.48 us (1%)
  other arithmetic  1.22 us (1%)
    all_gather x1, blocking collectives, on_device(): basis_rows = lax.all_gather(near_rows, 'far', axis=0).reshape(-1, rows)  39 us
    all_to_all x1, blocking collectives, on_device(): lax.all_to_all(partial_grad.reshape(n_data, tile_rows, hidden), DATA, 0, 0)  26.6 us
    all_to_all x1, starting transfers between devices, on_device(): pieces = lax.all_to_all(pieces, DATA, 0, 0)  14.7 us
    all_to_all x1, blocking collectives, spread(): return lax.all_to_all(jnp.broadcast_to(x[None], (n, *x.shape)), axes, 0, 0)  11.1 us
    pallas_call x1, Pallas kernels, whole_grad(): pl.pallas_call(grad_kernel, in_specs=[pl.BlockSpec(memory_space=pltpu.HBM...  6.82 us
    all_to_all x1, starting transfers between devices, spread(): return lax.all_to_all(jnp.broadcast_to(x[None], (n, *x.shape)), axes, 0, 0)  6.44 us
    all_gather x1, blocking collectives, on_device(): directions = lax.all_gather(spread(direction, CHIPS), 'core', axis=0)  4.42 us
  transfers between devices with their start and end apart: 2, of which 0 were waited for; matrix products, arithmetic and copies ran while one was open for 0% of the time, Pallas kernels for 6%

profile of v4, /device:TPU:1, one launch (start us, length us, event | category | flops | bytes accessed | tf_op | source)
XLA Modules:
  0.0 114.6 jit_solution(3756715821634462032)
XLA Ops:
  0.6 0.0 copy-start
  0.7 0.9 copy-done
  1.6 0.6 broadcast_in_dim.4
  2.2 6.4 %all-to-all-start = ((bf16[4,32,128]{2,1,0:T(8,128)(2,1)}), bf16[4,32,128]{2,1,0:T(8,128)(2,1)S(1)}, u32[]{:S(2)}, u32[]{:S(2)}) async-start(bf16[4,32,128]{2,1,0:T(8,128)(2,1)} %broadcast_in_dim.4), calls=%async_computation | async-start | bytes 65536 | tf_op jit(solution)/shard_map/all_to_all | solution.py:22
  8.7 6.8 %whole_grad.1 = bf16[32,344,128]{2,1,0:T(8,128)(2,1)} custom-call(bf16[344,1024]{1,0:T(8,128)(2,1)} %bitcast.16, bf16[1024,4096]{1,0:T(8,128)(2,1)} %act_hbm.1), custom_call_target="tpu_custom_call" | custom-call | tf_op jit(solution)/shard_map/whole_grad/pallas_call | solution.py:58
  15.5 0.0 all-to-all-done
  15.5 14.7 %all-to-all-start.1 = ((bf16[32,344,128]{2,1,0:T(8,128)(2,1)}), bf16[32,344,128]{2,1,0:T(8,128)(2,1)S(1)}, u32[]{:S(2)}, u32[]{:S(2)}) async-start(bf16[32,344,128]{2,1,0:T(8,128)(2,1)} %whole_grad.1), calls=%async_computation.1 | async-start | bytes 5636096 | tf_op jit(solution)/shard_map/all_to_all | solution.py:94
  30.2 39.0 %all-gather = bf16[32,32,128]{2,1,0:T(8,128)(2,1)S(1)} all-gather(bf16[4,32,128]{2,1,0:T(8,128)(2,1)S(1)} %all-to-all-done), channel_id=2, replica_groups=mesh['xl'=2,'y'=4,'core'=2,'far'=8,'near'=4,'xh'=2] {'far'}, dimensions={0}, use_global_device_ids=true | all-gather | bytes 294912 | tf_op jit(solution)/shard_map/all_gather | solution.py:92
  69.2 0.0 all-to-all-done.1
  69.2 0.4 convert_reduce_fusion
  69.7 0.0 copy-start.1
  69.7 0.0 copy-start.2
  69.7 0.4 convolution_convert_fusion
  70.1 0.4 copy.11
  70.4 26.6 %all_to_all.20 = bf16[32,32,344]{2,1,0:T(8,128)(2,1)S(1)} all-to-all(bf16[32,32,344]{2,1,0:T(8,128)(2,1)S(1)} %bitcast.12), channel_id=1, replica_groups=mesh['xl'=2,'y'=4,'core'=2,'far'=8,'near'=4,'xh'=2] {'xl','y','core','xh'}, dimensions={0} | all-to-all | bytes 1409024 | tf_op jit(solution)/shard_map/all_to_all | solution.py:103
  97.0 0.1 convert_reduce_fusion.1
  97.1 0.0 copy-done.1
  97.1 0.0 copy-done.2
  97.2 0.7 divide_convert_fusion
  97.9 11.1 %all_to_all.21 = bf16[16,32,344]{2,1,0:T(8,128)(2,1)S(1)} all-to-all(bf16[16,32,344]{2,1,0:T(8,128)(2,1)S(1)} %broadcast_in_dim.5), channel_id=1, replica_groups=mesh['xl'=2,'y'=4,'core'=2,'far'=8,'near'=4,'xh'=2] {'xl','y','xh'}, dimensions={0} | all-to-all | bytes 704512 | tf_op jit(solution)/shard_map/all_to_all | solution.py:22
  109.0 4.4 %all-gather.1 = bf16[32,32,344]{2,1,0:T(8,128)(2,1)S(1)} all-gather(bf16[16,32,344]{2,1,0:T(8,128)(2,1)S(1)} %all_to_all.21), channel_id=3, replica_groups=mesh['xl'=2,'y'=4,'core'=2,'far'=8,'near'=4,'xh'=2] {'core'}, dimensions={0}, use_global_device_ids=true | all-gather | bytes 1056768 | tf_op jit(solution)/shard_map/all_gather | solution.py:110
  113.4 0.1 copy.12
  113.5 1.1 convolution_multiply_fusion
  (3 shorter events, 0.1 us)
Async XLA Ops:
  0.6 1.0 copy-start
  2.2 13.3 %all-to-all-start = ((bf16[4,32,128]{2,1,0:T(8,128)(2,1)}), bf16[4,32,128]{2,1,0:T(8,128)(2,1)S(1)}, u32[]{:S(2)}, u32[]{:S(2)}) async-start(bf16[4,32,128]{2,1,0:T(8,128)(2,1)} %broadcast_in_dim.4), calls=%async_computation | async-start | bytes 65536 | tf_op jit(solution)/shard_map/all_to_all | solution.py:22
  15.5 53.7 %all-to-all-start.1 = ((bf16[32,344,128]{2,1,0:T(8,128)(2,1)}), bf16[32,344,128]{2,1,0:T(8,128)(2,1)S(1)}, u32[]{:S(2)}, u32[]{:S(2)}) async-start(bf16[32,344,128]{2,1,0:T(8,128)(2,1)} %whole_grad.1), calls=%async_computation.1 | async-start | bytes 5636096 | tf_op jit(solution)/shard_map/all_to_all | solution.py:94
  69.7 27.5 %copy-start.1 = (f32[32,344]{1,0:T(8,128)S(1)}, f32[32,344]{1,0:T(8,128)}, u32[]{:S(2)}) copy-start(f32[32,344]{1,0:T(8,128)} %param.9) | copy-start | bytes 132100
  69.7 27.5 %copy-start.2 = (f32[32,344]{1,0:T(8,128)S(1)}, f32[32,344]{1,0:T(8,128)}, u32[]{:S(2)}) copy-start(f32[32,344]{1,0:T(8,128)} %param.8) | copy-start | bytes 132100

commit v5 on v4

--- a/solution.py
+++ b/solution.py
@@ -79,28 +79,85 @@
     )
 
 
+def rows_kernel(basis_hbm, out_hbm, sem):
+    rows = out_hbm.shape[2]
+    here = pl.multiple_of(lax.axis_index(DATA) * rows, rows)
+    copies = [
+        pltpu.make_async_copy(basis_hbm.at[:, pl.ds(here, rows)], out_hbm.at[i], sem.at[i])
+        for i in range(out_hbm.shape[0])
+    ]
+    for copy in copies:
+        copy.start()
+    for copy in copies:
+        copy.wait()
+
+
+def own_rows(basis, rows):
+    n = lax.axis_size("near")
+    return pl.pallas_call(
+        rows_kernel,
+        in_specs=[pl.BlockSpec(memory_space=pltpu.HBM)],
+        out_specs=pl.BlockSpec(memory_space=pltpu.HBM),
+        out_shape=jax.ShapeDtypeStruct((n, basis.shape[0], rows), basis.dtype),
+        scratch_shapes=[pltpu.SemaphoreType.DMA((n,))],
+        name="own_rows",
+    )(pltpu.with_memory_space_constraint(basis, pltpu.HBM))
+
+
+def partial_kernel(pieces, basis, keep, send, partial):
+    total = pieces[0].astype(jnp.float32)
+    for i in range(1, pieces.shape[0]):
+        total += pieces[i].astype(jnp.float32)
+    high = total.astype(jnp.bfloat16)
+    low = (total - high.astype(jnp.float32)).astype(jnp.bfloat16)
+    over_rows = (((1,), (1,)), ((), ()))
+    partial[...] = lax.dot_general(
+        jnp.concatenate([basis[...], basis[...]], axis=1),
+        jnp.concatenate([high, low], axis=1),
+        over_rows,
+        preferred_element_type=jnp.float32,
+    )
+    core = lax.axis_index("core")
+    tiles, tile_rows = keep.shape[0], keep.shape[1]
+    for tile in range(tiles):
+        for ref, which in ((send, 1 - core), (keep, core)):
+            first = ((tile // 2 * 2 + which) * 2 + tile % 2) * tile_rows
+            ref[tile] = partial[pl.ds(pl.multiple_of(first, tile_rows), tile_rows), :].astype(
+                ref.dtype
+            )
+
+
+def partial_grad(pieces, basis, tile_rows):
+    tiles, hidden, ranks = pieces.shape[0] // 2, pieces.shape[1], basis.shape[0]
+    shape = (tiles, tile_rows, hidden)
+    return pl.pallas_call(
+        partial_kernel,
+        in_specs=[pl.BlockSpec(memory_space=pltpu.VMEM)] * 2,
+        out_specs=[pl.BlockSpec(memory_space=pltpu.VMEM)] * 2,
+        out_shape=[
+            jax.ShapeDtypeStruct(shape, jnp.float32),
+            jax.ShapeDtypeStruct(shape, jnp.bfloat16),
+        ],
+        scratch_shapes=[pltpu.VMEM((ranks, hidden), jnp.float32)],
+        compiler_params=pltpu.CompilerParams(vmem_limit_bytes=24 << 20),
+        name="partial_grad",
+    )(pieces, basis)
+
+
 def on_device(activations, cotangent, projection_basis, first_moment, second_moment):
     n_data = lax.axis_size(DATA)
-    here = lax.axis_index(DATA)
     width, own_rank = projection_basis.shape
     rows, tile_rows, hidden = width // n_data, first_moment.shape[0], cotangent.shape[1]
 
-    own_rows = lax.dynamic_slice_in_dim(projection_basis.T, here * rows, rows, 1)
-    near_rows = spread(own_rows, "near")
+    near_rows = lax.all_to_all(own_rows(projection_basis.T, rows), "near", 0, 0)
     pieces = whole_grad(cotangent.T, activations, n_data)
     pieces, near_rows = lax.optimization_barrier((pieces, near_rows))
     basis_rows = lax.all_gather(near_rows, "far", axis=0).reshape(-1, rows)
 
     pieces = lax.all_to_all(pieces, DATA, 0, 0)
-    grad_rows = jnp.sum(pieces.astype(jnp.float32), axis=0)
-    high = grad_rows.astype(jnp.bfloat16)
-    low = (grad_rows - high.astype(jnp.float32)).astype(jnp.bfloat16)
-    partial_grad = jnp.dot(
-        jnp.concatenate([basis_rows, basis_rows], axis=1),
-        jnp.concatenate([high, low], axis=1).T,
-        preferred_element_type=jnp.float32,
-    ).astype(jnp.bfloat16)
-    tiles = lax.all_to_all(partial_grad.reshape(n_data, tile_rows, hidden), DATA, 0, 0)
+    keep, send = partial_grad(pieces, basis_rows, tile_rows)
+    sent = lax.ppermute(send, "core", ((0, 1), (1, 0)))
+    tiles = lax.all_to_all((keep + sent.astype(jnp.float32)).astype(jnp.bfloat16), CHIPS, 0, 0)
     grad_tile = jnp.sum(tiles.astype(jnp.float32), axis=0)
     first_new = beta_first * first_moment + (1.0 - beta_first) * grad_tile
     second_new = beta_second * second_moment + (1.0 - beta_second) * grad_tile * grad_tile

time: 115 us -> 113 us (0.983)
  blocking collectives: 81.1 us -> 70.5 us
  starting transfers between devices: 21.2 us -> 28.5 us
  Pallas kernels: 6.82 us -> 10 us
  local copies, waits for them, and re-layouts: 2.05 us -> 0.13 us
  waiting for transfers between devices: 0.01 us -> 1.33 us
    all_to_all x1, blocking collectives: 26.6 us -> 14.8 us  [on_device(): lax.all_to_all((keep + sent.astype(jnp.float32)).astype(jnp.bfloat16), CH...]
    ppermute x0 -> x1, starting transfers between devices: none -> 7.29 us  [on_device(): sent = lax.ppermute(send, 'core', ((0, 1), (1, 0)))]
    pallas_call x0 -> x2, Pallas kernels: none -> 3.22 us  [the longest x1 2.15 us: own_rows(): pl.pallas_call(rows_kernel, in_specs=[pl.BlockSpec(memory_space=pltpu.HBM...]
    ppermute x0 -> x1, waiting for transfers between devices: none -> 1.33 us  [on_device(): sent = lax.ppermute(send, 'core', ((0, 1), (1, 0)))]
  transfers between devices with their start and end apart: 2 -> 3, of which waited for: 0 -> 1; matrix products, arithmetic and copies ran while one was open for 0% -> 0% of each run, Pallas kernels for 6% -> 6%
where the time goes in v5:
time: 113 us
  blocking collectives  70.5 us (62%)
  starting transfers between devices  28.5 us (25%)
  Pallas kernels  10 us (9%)
  waiting for transfers between devices  1.33 us (1%)
    all_gather x1, blocking collectives, on_device(): basis_rows = lax.all_gather(near_rows, 'far', axis=0).reshape(-1, rows)  39 us
    all_to_all x1, blocking collectives, on_device(): lax.all_to_all((keep + sent.astype(jnp.float32)).astype(jnp.bfloat16), CH...  14.8 us
    all_to_all x1, starting transfers between devices, on_device(): pieces = lax.all_to_all(pieces, DATA, 0, 0)  14.7 us
    all_to_all x1, blocking collectives, spread(): return lax.all_to_all(jnp.broadcast_to(x[None], (n, *x.shape)), axes, 0, 0)  11.7 us
    ppermute x1, starting transfers between devices, on_device(): sent = lax.ppermute(send, 'core', ((0, 1), (1, 0)))  7.29 us
    pallas_call x1, Pallas kernels, whole_grad(): pl.pallas_call(grad_kernel, in_specs=[pl.BlockSpec(memory_space=pltpu.HBM...  6.83 us
    all_to_all x1, starting transfers between devices, on_device(): near_rows = lax.all_to_all(own_rows(projection_basis.T, rows), 'near', 0, 0)  6.46 us
    all_gather x1, blocking collectives, on_device(): directions = lax.all_gather(spread(direction, CHIPS), 'core', axis=0)  4.96 us
  transfers between devices with their start and end apart: 3, of which 1 were waited for; matrix products, arithmetic and copies ran while one was open for 0% of the time, Pallas kernels for 6%

profile of v5, /device:TPU:1, one launch (start us, length us, event | category | flops | bytes accessed | tf_op | source)
XLA Modules:
  0.0 113.1 jit_solution(17015101934208965230)
XLA Ops:
  0.6 2.1 %own_rows.1 = bf16[4,32,128]{2,1,0:T(8,128)(2,1)} custom-call(bf16[32,4096]{1,0:T(8,128)(2,1)} %bitcast.14), custom_call_target="tpu_custom_call" | custom-call | tf_op jit(solution)/shard_map/own_rows/pallas_call | solution.py:97
  2.8 6.5 %all-to-all-start = ((bf16[4,32,128]{2,1,0:T(8,128)(2,1)}), bf16[4,32,128]{2,1,0:T(8,128)(2,1)S(1)}, u32[]{:S(2)}, u32[]{:S(2)}) async-start(bf16[4,32,128]{2,1,0:T(8,128)(2,1)} %own_rows.1), calls=%async_computation | async-start | bytes 65536 | tf_op jit(solution)/shard_map/all_to_all | solution.py:152
  9.2 6.8 %whole_grad.1 = bf16[32,344,128]{2,1,0:T(8,128)(2,1)} custom-call(bf16[344,1024]{1,0:T(8,128)(2,1)} %bitcast.13, bf16[1024,4096]{1,0:T(8,128)(2,1)} %act_hbm.1), custom_call_target="tpu_custom_call" | custom-call | tf_op jit(solution)/shard_map/whole_grad/pallas_call | solution.py:58
  16.1 0.0 all-to-all-done
  16.1 14.7 %all-to-all-start.1 = ((bf16[32,344,128]{2,1,0:T(8,128)(2,1)}), bf16[32,344,128]{2,1,0:T(8,128)(2,1)S(1)}, u32[]{:S(2)}, u32[]{:S(2)}) async-start(bf16[32,344,128]{2,1,0:T(8,128)(2,1)} %whole_grad.1), calls=%async_computation.1 | async-start | bytes 5636096 | tf_op jit(solution)/shard_map/all_to_all | solution.py:157
  30.8 39.0 %all-gather = bf16[32,32,128]{2,1,0:T(8,128)(2,1)S(1)} all-gather(bf16[4,32,128]{2,1,0:T(8,128)(2,1)S(1)} %all-to-all-done), channel_id=2, replica_groups=mesh['xl'=2,'y'=4,'core'=2,'far'=8,'near'=4,'xh'=2] {'far'}, dimensions={0}, use_global_device_ids=true | all-gather | bytes 294912 | tf_op jit(solution)/shard_map/all_gather | solution.py:155
  69.8 0.0 all-to-all-done.1.pieces
  69.8 0.0 copy-start
  69.8 0.0 copy-start.1
  69.9 1.1 partial_grad.1
  70.9 7.3 %collective-permute-start = (bf16[16,32,344]{2,1,0:T(8,128)(2,1)S(1)}, bf16[16,32,344]{2,1,0:T(8,128)(2,1)S(1)}, u32[]{:S(2)}, u32[]{:S(2)}) collective-permute-start(bf16[16,32,344]{2,1,0:T(8,128)(2,1)S(1)} %get-tuple-element.10), channel_id=1, source_target_pairs={{0,64},{64,0},{1,65},{65,1},{2,66},{66,2},{3,67},{67,3},{4,68},{68... | collective-permute-start | bytes 1056776 | tf_op jit(solution)/shard_map/ppermute | solution.py:159
  78.2 1.3 %collective-permute-done = bf16[16,32,344]{2,1,0:T(8,128)(2,1)S(1)} collective-permute-done((bf16[16,32,344]{2,1,0:T(8,128)(2,1)S(1)}, bf16[16,32,344]{2,1,0:T(8,128)(2,1)S(1)}, u32[]{:S(2)}, u32[]{:S(2)}) %collective-permute-start) | collective-permute-done | bytes 352288 | tf_op jit(solution)/shard_map/ppermute | solution.py:159
  79.5 0.1 add_convert_fusion
  79.6 14.8 %all_to_all.20 = bf16[16,32,344]{2,1,0:T(8,128)(2,1)S(1)} all-to-all(bf16[16,32,344]{2,1,0:T(8,128)(2,1)S(1)} %add_convert_fusion), channel_id=1, replica_groups=mesh['xl'=2,'y'=4,'core'=2,'far'=8,'near'=4,'xh'=2] {'xl','y','xh'}, dimensions={0} | all-to-all | bytes 704512 | tf_op jit(solution)/shard_map/all_to_all | solution.py:160
  94.4 0.1 convert_reduce_fusion
  94.5 0.0 copy-done
  94.5 0.0 copy-done.1
  94.5 0.7 divide_convert_fusion
  95.2 11.7 %all_to_all.21 = bf16[16,32,344]{2,1,0:T(8,128)(2,1)S(1)} all-to-all(bf16[16,32,344]{2,1,0:T(8,128)(2,1)S(1)} %broadcast_in_dim.2), channel_id=1, replica_groups=mesh['xl'=2,'y'=4,'core'=2,'far'=8,'near'=4,'xh'=2] {'xl','y','xh'}, dimensions={0} | all-to-all | bytes 704512 | tf_op jit(solution)/shard_map/all_to_all | solution.py:22
  106.9 5.0 %all-gather.1 = bf16[32,32,344]{2,1,0:T(8,128)(2,1)S(1)} all-gather(bf16[16,32,344]{2,1,0:T(8,128)(2,1)S(1)} %all_to_all.21), channel_id=3, replica_groups=mesh['xl'=2,'y'=4,'core'=2,'far'=8,'near'=4,'xh'=2] {'core'}, dimensions={0}, use_global_device_ids=true | all-gather | bytes 1056768 | tf_op jit(solution)/shard_map/all_gather | solution.py:167
  111.9 0.1 copy.9
  112.0 1.1 convolution_multiply_fusion
  (1 shorter events, 0.0 us)
Async XLA Ops:
  2.8 13.3 %all-to-all-start = ((bf16[4,32,128]{2,1,0:T(8,128)(2,1)}), bf16[4,32,128]{2,1,0:T(8,128)(2,1)S(1)}, u32[]{:S(2)}, u32[]{:S(2)}) async-start(bf16[4,32,128]{2,1,0:T(8,128)(2,1)} %own_rows.1), calls=%async_computation | async-start | bytes 65536 | tf_op jit(solution)/shard_map/all_to_all | solution.py:152
  16.1 53.8 %all-to-all-start.1 = ((bf16[32,344,128]{2,1,0:T(8,128)(2,1)}), bf16[32,344,128]{2,1,0:T(8,128)(2,1)S(1)}, u32[]{:S(2)}, u32[]{:S(2)}) async-start(bf16[32,344,128]{2,1,0:T(8,128)(2,1)} %whole_grad.1), calls=%async_computation.1 | async-start | bytes 5636096 | tf_op jit(solution)/shard_map/all_to_all | solution.py:157
  69.8 24.6 %copy-start = (f32[32,344]{1,0:T(8,128)S(1)}, f32[32,344]{1,0:T(8,128)}, u32[]{:S(2)}) copy-start(f32[32,344]{1,0:T(8,128)} %param.9) | copy-start | bytes 132100
  69.8 24.6 %copy-start.1 = (f32[32,344]{1,0:T(8,128)S(1)}, f32[32,344]{1,0:T(8,128)}, u32[]{:S(2)}) copy-start(f32[32,344]{1,0:T(8,128)} %param.8) | copy-start | bytes 132100
  70.9 8.6 %collective-permute-start = (bf16[16,32,344]{2,1,0:T(8,128)(2,1)S(1)}, bf16[16,32,344]{2,1,0:T(8,128)(2,1)S(1)}, u32[]{:S(2)}, u32[]{:S(2)}) collective-permute-start(bf16[16,32,344]{2,1,0:T(8,128)(2,1)S(1)} %get-tuple-element.10), channel_id=1, source_target_pairs={{0,64},{64,0},{1,65},{65,1},{2,66},{66,2},{3,67},{67,3},{4,68},{68... | collective-permute-start | bytes 1056776 | tf_op jit(solution)/shard_map/ppermute | solution.py:159

commit v6 on v5

--- a/solution.py
+++ b/solution.py
@@ -22,86 +22,99 @@
     return lax.all_to_all(jnp.broadcast_to(x[None], (n, *x.shape)), axes, 0, 0)
 
 
-def grad_kernel(cot_hbm, act_hbm, out_hbm, cot, act, out, cot_sem, in_sem, out_sem):
+def in_hbm(x):
+    return pltpu.with_memory_space_constraint(x, pltpu.HBM)
+
+
+def stage_kernel(basis_hbm, cot_hbm, act_hbm, rows_hbm, cot, act, sem, act_sem):
+    n, _, rows = rows_hbm.shape
+    here = pl.multiple_of(lax.axis_index(DATA) * rows, rows)
+    copies = [
+        pltpu.make_async_copy(basis_hbm.at[:, pl.ds(here, rows)], rows_hbm.at[i], sem.at[i])
+        for i in range(n)
+    ]
+    copies.append(pltpu.make_async_copy(act_hbm.at[:, : act.shape[1]], act, act_sem.at[0]))
+    copies.append(pltpu.make_async_copy(cot_hbm, cot, act_sem.at[1]))
+    for copy in copies:
+        copy.start()
+    for copy in copies:
+        copy.wait()
+
+
+def stage(basis, cotangent, activations, rows):
+    n, (tokens, width) = lax.axis_size("near"), activations.shape
+    return pl.pallas_call(
+        stage_kernel,
+        in_specs=[pl.BlockSpec(memory_space=pltpu.HBM)] * 3,
+        out_specs=[
+            pl.BlockSpec(memory_space=pltpu.HBM),
+            pl.BlockSpec(memory_space=pltpu.VMEM),
+            pl.BlockSpec(memory_space=pltpu.VMEM),
+        ],
+        out_shape=[
+            pltpu.HBM((n, basis.shape[0], rows), basis.dtype),
+            pltpu.VMEM(cotangent.shape, cotangent.dtype),
+            pltpu.VMEM((tokens, width // 4), activations.dtype),
+        ],
+        scratch_shapes=[pltpu.SemaphoreType.DMA((n,)), pltpu.SemaphoreType.DMA((2,))],
+        compiler_params=pltpu.CompilerParams(vmem_limit_bytes=16 << 20),
+        name="stage",
+    )(in_hbm(basis), in_hbm(cotangent), in_hbm(activations))
+
+
+def grad_kernel(cot, first, act_hbm, out_hbm, second, third, out, in_sem, out_sem):
     chunks, per_chunk, width = out.shape[0], out.shape[1], out.shape[3]
     cols = per_chunk * width
-
-    def fetch(c):
-        return pltpu.make_async_copy(
-            act_hbm.at[:, c * cols : (c + 1) * cols], act.at[c], in_sem.at[c]
-        )
 
     def send(c):
         return pltpu.make_async_copy(
             out.at[c], out_hbm.at[c * per_chunk : (c + 1) * per_chunk], out_sem.at[c]
         )
 
-    whole = pltpu.make_async_copy(cot_hbm, cot, cot_sem)
-    whole.start()
-    for c in range(chunks):
-        fetch(c).start()
-    whole.wait()
-    for c in range(chunks):
-        fetch(c).wait()
-        block = jnp.dot(cot[...], act[c], preferred_element_type=jnp.float32)
-        for p in range(per_chunk):
-            out[c, p] = block[:, p * width : (p + 1) * width].astype(out.dtype)
-        send(c).start()
+    fetches, at = {}, first.shape[1]
+    for i, act in enumerate((second, third)):
+        fetches[at] = pltpu.make_async_copy(
+            act_hbm.at[:, at : at + act.shape[1]], act, in_sem.at[i]
+        )
+        fetches[at].start()
+        at += act.shape[1]
+    at = 0
+    for act in (first, second, third):
+        if at in fetches:
+            fetches[at].wait()
+        for lo in range(0, act.shape[1], cols):
+            block = jnp.dot(cot[...], act[:, lo : lo + cols], preferred_element_type=jnp.float32)
+            c = (at + lo) // cols
+            for p in range(per_chunk):
+                out[c, p] = block[:, p * width : (p + 1) * width].astype(out.dtype)
+            send(c).start()
+        at += act.shape[1]
     for c in range(chunks):
         send(c).wait()
 
 
-def whole_grad(cotangent, activations, pieces, chunks=2):
-    tokens, width = activations.shape
-    hidden, cols = cotangent.shape[0], width // pieces
-    per_chunk = pieces // chunks
+def whole_grad(cotangent, first, activations, pieces, chunks=8):
+    hidden, (tokens, width) = cotangent.shape[0], activations.shape
+    done, cols, dtype = first.shape[1], width // pieces, activations.dtype
     return pl.pallas_call(
         grad_kernel,
         in_specs=[
+            pl.BlockSpec(memory_space=pltpu.VMEM),
+            pl.BlockSpec(memory_space=pltpu.VMEM),
             pl.BlockSpec(memory_space=pltpu.HBM),
-            pl.BlockSpec(memory_space=pltpu.HBM),
         ],
         out_specs=pl.BlockSpec(memory_space=pltpu.HBM),
-        out_shape=jax.ShapeDtypeStruct((pieces, hidden, cols), jnp.bfloat16),
+        out_shape=pltpu.HBM((pieces, hidden, cols), jnp.bfloat16),
         scratch_shapes=[
-            pltpu.VMEM(cotangent.shape, cotangent.dtype),
-            pltpu.VMEM((chunks, tokens, per_chunk * cols), jnp.bfloat16),
-            pltpu.VMEM((chunks, per_chunk, hidden, cols), jnp.bfloat16),
-            pltpu.SemaphoreType.DMA,
+            pltpu.VMEM((tokens, done), dtype),
+            pltpu.VMEM((tokens, width - 2 * done), dtype),
+            pltpu.VMEM((chunks, pieces // chunks, hidden, cols), jnp.bfloat16),
+            pltpu.SemaphoreType.DMA((2,)),
             pltpu.SemaphoreType.DMA((chunks,)),
-            pltpu.SemaphoreType.DMA((chunks,)),
-        ],
-        compiler_params=pltpu.CompilerParams(vmem_limit_bytes=40 << 20),
+        ],
+        compiler_params=pltpu.CompilerParams(vmem_limit_bytes=24 << 20),
         name="whole_grad",
-    )(
-        pltpu.with_memory_space_constraint(cotangent, pltpu.HBM),
-        pltpu.with_memory_space_constraint(activations, pltpu.HBM),
-    )
-
-
-def rows_kernel(basis_hbm, out_hbm, sem):
-    rows = out_hbm.shape[2]
-    here = pl.multiple_of(lax.axis_index(DATA) * rows, rows)
-    copies = [
-        pltpu.make_async_copy(basis_hbm.at[:, pl.ds(here, rows)], out_hbm.at[i], sem.at[i])
-        for i in range(out_hbm.shape[0])
-    ]
-    for copy in copies:
-        copy.start()
-    for copy in copies:
-        copy.wait()
-
-
-def own_rows(basis, rows):
-    n = lax.axis_size("near")
-    return pl.pallas_call(
-        rows_kernel,
-        in_specs=[pl.BlockSpec(memory_space=pltpu.HBM)],
-        out_specs=pl.BlockSpec(memory_space=pltpu.HBM),
-        out_shape=jax.ShapeDtypeStruct((n, basis.shape[0], rows), basis.dtype),
-        scratch_shapes=[pltpu.SemaphoreType.DMA((n,))],
-        name="own_rows",
-    )(pltpu.with_memory_space_constraint(basis, pltpu.HBM))
+    )(cotangent, first, in_hbm(activations))
 
 
 def partial_kernel(pieces, basis, keep, send, partial):
@@ -149,8 +162,9 @@
     width, own_rank = projection_basis.shape
     rows, tile_rows, hidden = width // n_data, first_moment.shape[0], cotangent.shape[1]
 
-    near_rows = lax.all_to_all(own_rows(projection_basis.T, rows), "near", 0, 0)
-    pieces = whole_grad(cotangent.T, activations, n_data)
+    own_rows, cot, first = stage(projection_basis.T, cotangent.T, activations, rows)
+    near_rows = lax.all_to_all(own_rows, "near", 0, 0)
+    pieces = whole_grad(cot, first, activations, n_data)
     pieces, near_rows = lax.optimization_barrier((pieces, near_rows))
     basis_rows = lax.all_gather(near_rows, "far", axis=0).reshape(-1, rows)
 

time: 113 us -> 113 us (level)
  transfers between devices with their start and end apart: 3 -> 3, of which waited for: 1 -> 1; matrix products, arithmetic and copies ran while one was open for 0% -> 0% of each run, Pallas kernels for 6% -> 5%
where the time goes in v6:
time: 113 us
  blocking collectives  70.8 us (63%)
  starting transfers between devices  28.4 us (25%)
  Pallas kernels  9.35 us (8%)
  waiting for transfers between devices  1.33 us (1%)
    all_gather x1, blocking collectives, on_device(): basis_rows = lax.all_gather(near_rows, 'far', axis=0).reshape(-1, rows)  39 us
    all_to_all x1, blocking collectives, on_device(): lax.all_to_all((keep + sent.astype(jnp.float32)).astype(jnp.bfloat16), CH...  15 us
    all_to_all x1, starting transfers between devices, on_device(): pieces = lax.all_to_all(pieces, DATA, 0, 0)  14.7 us
    all_to_all x1, blocking collectives, spread(): return lax.all_to_all(jnp.broadcast_to(x[None], (n, *x.shape)), axes, 0, 0)  11.7 us
    ppermute x1, starting transfers between devices, on_device(): sent = lax.ppermute(send, 'core', ((0, 1), (1, 0)))  7.26 us
    all_to_all x1, starting transfers between devices, on_device(): near_rows = lax.all_to_all(own_rows, 'near', 0, 0)  6.46 us
    pallas_call x1, Pallas kernels, whole_grad(): pl.pallas_call(grad_kernel, in_specs=[pl.BlockSpec(memory_space=pltpu.VME...  6.11 us
    all_gather x1, blocking collectives, on_device(): directions = lax.all_gather(spread(direction, CHIPS), 'core', axis=0)  4.96 us
  transfers between devices with their start and end apart: 3, of which 1 were waited for; matrix products, arithmetic and copies ran while one was open for 0% of the time, Pallas kernels for 5%

profile of v6, /device:TPU:1, one launch (start us, length us, event | category | flops | bytes accessed | tf_op | source)
XLA Modules:
  0.0 112.6 jit_solution(5204932238813800240)
XLA Ops:
  0.6 2.2 %stage.1 = (bf16[4,32,128]{2,1,0:T(8,128)(2,1)}, bf16[344,1024]{1,0:T(8,128)(2,1)S(1)}, bf16[1024,1024]{1,0:T(8,128)(2,1)S(1)}) custom-call(bf16[32,4096]{1,0:T(8,128)(2,1)} %bitcast.14, bf16[344,1024]{1,0:T(8,128)(2,1)} %bitcast.13, bf16[1024,4096]{1,0:T(8,128)(2,1)} %act_hbm.3), custom_call_target="tpu_custom_call" | custom-call | tf_op jit(solution)/shard_map/stage/pallas_call | solution.py:46
  2.8 6.5 %all-to-all-start = ((bf16[4,32,128]{2,1,0:T(8,128)(2,1)}), bf16[4,32,128]{2,1,0:T(8,128)(2,1)S(1)}, u32[]{:S(2)}, u32[]{:S(2)}) async-start(bf16[4,32,128]{2,1,0:T(8,128)(2,1)} %get-tuple-element.12), calls=%async_computation | async-start | bytes 65536 | tf_op jit(solution)/shard_map/all_to_all | solution.py:166
  9.3 6.1 %whole_grad.1 = bf16[32,344,128]{2,1,0:T(8,128)(2,1)} custom-call(bf16[344,1024]{1,0:T(8,128)(2,1)S(1)} %get-tuple-element.10.cot, bf16[1024,1024]{1,0:T(8,128)(2,1)S(1)} %get-tuple-element.11.first, bf16[1024,4096]{1,0:T(8,128)(2,1)} %act_hbm.3), custom_call_target="tpu_custom_call" | custom-call | tf_op jit(solution)/shard_map/whole_grad/pallas_call | solution.py:99
  15.4 0.0 all-to-all-done
  15.4 14.7 %all-to-all-start.1 = ((bf16[32,344,128]{2,1,0:T(8,128)(2,1)}), bf16[32,344,128]{2,1,0:T(8,128)(2,1)S(1)}, u32[]{:S(2)}, u32[]{:S(2)}) async-start(bf16[32,344,128]{2,1,0:T(8,128)(2,1)} %whole_grad.1), calls=%async_computation.1 | async-start | bytes 5636096 | tf_op jit(solution)/shard_map/all_to_all | solution.py:171
  30.1 39.0 %all-gather = bf16[32,32,128]{2,1,0:T(8,128)(2,1)S(1)} all-gather(bf16[4,32,128]{2,1,0:T(8,128)(2,1)S(1)} %all-to-all-done), channel_id=2, replica_groups=mesh['xl'=2,'y'=4,'core'=2,'far'=8,'near'=4,'xh'=2] {'far'}, dimensions={0}, use_global_device_ids=true | all-gather | bytes 294912 | tf_op jit(solution)/shard_map/all_gather | solution.py:169
  69.1 0.0 all-to-all-done.1.pieces
  69.2 0.0 copy-start
  69.2 0.0 copy-start.1
  69.2 1.1 partial_grad.1
  70.2 7.3 %collective-permute-start = (bf16[16,32,344]{2,1,0:T(8,128)(2,1)S(1)}, bf16[16,32,344]{2,1,0:T(8,128)(2,1)S(1)}, u32[]{:S(2)}, u32[]{:S(2)}) collective-permute-start(bf16[16,32,344]{2,1,0:T(8,128)(2,1)S(1)} %get-tuple-element.16), channel_id=1, source_target_pairs={{0,64},{64,0},{1,65},{65,1},{2,66},{66,2},{3,67},{67,3},{4,68},{68... | collective-permute-start | bytes 1056776 | tf_op jit(solution)/shard_map/ppermute | solution.py:173
  77.5 1.3 %collective-permute-done = bf16[16,32,344]{2,1,0:T(8,128)(2,1)S(1)} collective-permute-done((bf16[16,32,344]{2,1,0:T(8,128)(2,1)S(1)}, bf16[16,32,344]{2,1,0:T(8,128)(2,1)S(1)}, u32[]{:S(2)}, u32[]{:S(2)}) %collective-permute-start) | collective-permute-done | bytes 352288 | tf_op jit(solution)/shard_map/ppermute | solution.py:173
  78.8 0.1 add_convert_fusion
  78.9 15.0 %all_to_all.20 = bf16[16,32,344]{2,1,0:T(8,128)(2,1)S(1)} all-to-all(bf16[16,32,344]{2,1,0:T(8,128)(2,1)S(1)} %add_convert_fusion), channel_id=1, replica_groups=mesh['xl'=2,'y'=4,'core'=2,'far'=8,'near'=4,'xh'=2] {'xl','y','xh'}, dimensions={0} | all-to-all | bytes 704512 | tf_op jit(solution)/shard_map/all_to_all | solution.py:174
  94.0 0.1 convert_reduce_fusion
  94.0 0.0 copy-done
  94.0 0.0 copy-done.1
  94.0 0.7 divide_convert_fusion
  94.7 11.7 %all_to_all.21 = bf16[16,32,344]{2,1,0:T(8,128)(2,1)S(1)} all-to-all(bf16[16,32,344]{2,1,0:T(8,128)(2,1)S(1)} %broadcast_in_dim.2), channel_id=1, replica_groups=mesh['xl'=2,'y'=4,'core'=2,'far'=8,'near'=4,'xh'=2] {'xl','y','xh'}, dimensions={0} | all-to-all | bytes 704512 | tf_op jit(solution)/shard_map/all_to_all | solution.py:22
  106.5 5.0 %all-gather.1 = bf16[32,32,344]{2,1,0:T(8,128)(2,1)S(1)} all-gather(bf16[16,32,344]{2,1,0:T(8,128)(2,1)S(1)} %all_to_all.21), channel_id=3, replica_groups=mesh['xl'=2,'y'=4,'core'=2,'far'=8,'near'=4,'xh'=2] {'core'}, dimensions={0}, use_global_device_ids=true | all-gather | bytes 1056768 | tf_op jit(solution)/shard_map/all_gather | solution.py:181
  111.4 0.1 copy.9
  111.5 1.1 convolution_multiply_fusion
  (1 shorter events, 0.0 us)
Async XLA Ops:
  2.8 12.6 %all-to-all-start = ((bf16[4,32,128]{2,1,0:T(8,128)(2,1)}), bf16[4,32,128]{2,1,0:T(8,128)(2,1)S(1)}, u32[]{:S(2)}, u32[]{:S(2)}) async-start(bf16[4,32,128]{2,1,0:T(8,128)(2,1)} %get-tuple-element.12), calls=%async_computation | async-start | bytes 65536 | tf_op jit(solution)/shard_map/all_to_all | solution.py:166
  15.4 53.8 %all-to-all-start.1 = ((bf16[32,344,128]{2,1,0:T(8,128)(2,1)}), bf16[32,344,128]{2,1,0:T(8,128)(2,1)S(1)}, u32[]{:S(2)}, u32[]{:S(2)}) async-start(bf16[32,344,128]{2,1,0:T(8,128)(2,1)} %whole_grad.1), calls=%async_computation.1 | async-start | bytes 5636096 | tf_op jit(solution)/shard_map/all_to_all | solution.py:171
  69.2 24.9 %copy-start = (f32[32,344]{1,0:T(8,128)S(1)}, f32[32,344]{1,0:T(8,128)}, u32[]{:S(2)}) copy-start(f32[32,344]{1,0:T(8,128)} %param.9) | copy-start | bytes 132100
  69.2 24.9 %copy-start.1 = (f32[32,344]{1,0:T(8,128)S(1)}, f32[32,344]{1,0:T(8,128)}, u32[]{:S(2)}) copy-start(f32[32,344]{1,0:T(8,128)} %param.8) | copy-start | bytes 132100
  70.2 8.6 %collective-permute-start = (bf16[16,32,344]{2,1,0:T(8,128)(2,1)S(1)}, bf16[16,32,344]{2,1,0:T(8,128)(2,1)S(1)}, u32[]{:S(2)}, u32[]{:S(2)}) collective-permute-start(bf16[16,32,344]{2,1,0:T(8,128)(2,1)S(1)} %get-tuple-element.16), channel_id=1, source_target_pairs={{0,64},{64,0},{1,65},{65,1},{2,66},{66,2},{3,67},{67,3},{4,68},{68... | collective-permute-start | bytes 1056776 | tf_op jit(solution)/shard_map/ppermute | solution.py:173

commit v7 on v6

--- a/solution.py
+++ b/solution.py
@@ -26,18 +26,22 @@
     return pltpu.with_memory_space_constraint(x, pltpu.HBM)
 
 
-def stage_kernel(basis_hbm, cot_hbm, act_hbm, rows_hbm, cot, act, sem, act_sem):
+def stage_kernel(basis_hbm, cot_hbm, act_hbm, rows_hbm, cot, act, own, sem, in_sem):
     n, _, rows = rows_hbm.shape
     here = pl.multiple_of(lax.axis_index(DATA) * rows, rows)
-    copies = [
-        pltpu.make_async_copy(basis_hbm.at[:, pl.ds(here, rows)], rows_hbm.at[i], sem.at[i])
-        for i in range(n)
+    cut = pltpu.make_async_copy(basis_hbm.at[:, pl.ds(here, rows)], own, in_sem.at[0])
+    cut.start()
+    fetches = [
+        pltpu.make_async_copy(act_hbm.at[:, : act.shape[1]], act, in_sem.at[1]),
+        pltpu.make_async_copy(cot_hbm, cot, in_sem.at[2]),
     ]
-    copies.append(pltpu.make_async_copy(act_hbm.at[:, : act.shape[1]], act, act_sem.at[0]))
-    copies.append(pltpu.make_async_copy(cot_hbm, cot, act_sem.at[1]))
+    for fetch in fetches:
+        fetch.start()
+    cut.wait()
+    copies = [pltpu.make_async_copy(own, rows_hbm.at[i], sem.at[i]) for i in range(n)]
     for copy in copies:
         copy.start()
-    for copy in copies:
+    for copy in copies + fetches:
         copy.wait()
 
 
@@ -56,7 +60,11 @@
             pltpu.VMEM(cotangent.shape, cotangent.dtype),
             pltpu.VMEM((tokens, width // 4), activations.dtype),
         ],
-        scratch_shapes=[pltpu.SemaphoreType.DMA((n,)), pltpu.SemaphoreType.DMA((2,))],
+        scratch_shapes=[
+            pltpu.VMEM((basis.shape[0], rows), basis.dtype),
+            pltpu.SemaphoreType.DMA((n,)),
+            pltpu.SemaphoreType.DMA((3,)),
+        ],
         compiler_params=pltpu.CompilerParams(vmem_limit_bytes=16 << 20),
         name="stage",
     )(in_hbm(basis), in_hbm(cotangent), in_hbm(activations))
@@ -190,7 +198,7 @@
 def solution(mesh):
     dp, mp, pipe = mesh.devices.shape
     fine = Mesh(
-        mesh.devices.reshape(2, dp // 4, 2, mp // 4, 4, pipe),
+        mesh.devices.reshape(2, dp // 4, 2, mp // 8, 8, pipe),
         ("xl", "y", "core", "far", "near", "xh"),
     )
     return jax.shard_map(

time: 113 us -> 118 us (1.044)
  blocking collectives: 70.8 us -> 74.8 us
  waiting for transfers between devices: 1.33 us -> 4.97 us
  starting transfers between devices: 28.4 us -> 25.5 us
    all_to_all x1, starting transfers between devices: 6.46 us -> 13.1 us  [on_device(): near_rows = lax.all_to_all(own_rows, 'near', 0, 0)]
    all_to_all x1, starting transfers between devices: 14.7 us -> 9.25 us  [on_device(): pieces = lax.all_to_all(pieces, DATA, 0, 0)]
    ppermute x1, starting transfers between devices: 7.26 us -> 3.2 us  [on_device(): sent = lax.ppermute(send, 'core', ((0, 1), (1, 0)))]
    all_gather x1, blocking collectives: 39 us -> 43 us  [on_device(): basis_rows = lax.all_gather(near_rows, 'far', axis=0).reshape(-1, rows)]
    all_to_all x1, waiting for transfers between devices: 0.01 us -> 3.64 us  [on_device(): near_rows = lax.all_to_all(own_rows, 'near', 0, 0)]
  transfers between devices with their start and end apart: 3 -> 3, of which waited for: 1 -> 2; matrix products, arithmetic and copies ran while one was open for 0% -> 0% of each run, Pallas kernels for 5% -> 5%
where the time goes in v7:
time: 118 us; the launch traced here: 117 us
  blocking collectives  74.8 us (63%)
  starting transfers between devices  25.5 us (22%)
  Pallas kernels  9.08 us (8%)
  waiting for transfers between devices  4.97 us (4%)
    all_gather x1, blocking collectives, on_device(): basis_rows = lax.all_gather(near_rows, 'far', axis=0).reshape(-1, rows)  43 us
    all_to_all x1, blocking collectives, on_device(): lax.all_to_all((keep + sent.astype(jnp.float32)).astype(jnp.bfloat16), CH...  15 us
    all_to_all x1, starting transfers between devices, on_device(): near_rows = lax.all_to_all(own_rows, 'near', 0, 0)  13.1 us
    all_to_all x1, blocking collectives, spread(): return lax.all_to_all(jnp.broadcast_to(x[None], (n, *x.shape)), axes, 0, 0)  11.7 us
    all_to_all x1, starting transfers between devices, on_device(): pieces = lax.all_to_all(pieces, DATA, 0, 0)  9.25 us
    pallas_call x1, Pallas kernels, whole_grad(): pl.pallas_call(grad_kernel, in_specs=[pl.BlockSpec(memory_space=pltpu.VME...  6.11 us
    all_gather x1, blocking collectives, on_device(): directions = lax.all_gather(spread(direction, CHIPS), 'core', axis=0)  4.96 us
    all_to_all x1, waiting for transfers between devices, on_device(): near_rows = lax.all_to_all(own_rows, 'near', 0, 0)  3.64 us
  transfers between devices with their start and end apart: 3, of which 2 were waited for; matrix products, arithmetic and copies ran while one was open for 0% of the time, Pallas kernels for 5%

profile of v7, /device:TPU:1, one launch (start us, length us, event | category | flops | bytes accessed | tf_op | source)
XLA Modules:
  0.0 117.1 jit_solution(7001665521612279640)
XLA Ops:
  0.6 1.9 %stage.1 = (bf16[8,32,128]{2,1,0:T(8,128)(2,1)}, bf16[344,1024]{1,0:T(8,128)(2,1)S(1)}, bf16[1024,1024]{1,0:T(8,128)(2,1)S(1)}) custom-call(bf16[32,4096]{1,0:T(8,128)(2,1)} %bitcast.14, bf16[344,1024]{1,0:T(8,128)(2,1)} %bitcast.13, bf16[1024,4096]{1,0:T(8,128)(2,1)} %act_hbm.3), custom_call_target="tpu_custom_call" | custom-call | tf_op jit(solution)/shard_map/stage/pallas_call | solution.py:50
  2.5 13.1 %all-to-all-start = ((bf16[8,32,128]{2,1,0:T(8,128)(2,1)}), bf16[8,32,128]{2,1,0:T(8,128)(2,1)S(1)}, u32[]{:S(2)}, u32[]{:S(2)}) async-start(bf16[8,32,128]{2,1,0:T(8,128)(2,1)} %get-tuple-element.12), calls=%async_computation | async-start | bytes 131072 | tf_op jit(solution)/shard_map/all_to_all | solution.py:174
  15.6 6.1 %whole_grad.1 = bf16[32,344,128]{2,1,0:T(8,128)(2,1)} custom-call(bf16[344,1024]{1,0:T(8,128)(2,1)S(1)} %get-tuple-element.10.cot, bf16[1024,1024]{1,0:T(8,128)(2,1)S(1)} %get-tuple-element.11.first, bf16[1024,4096]{1,0:T(8,128)(2,1)} %act_hbm.3), custom_call_target="tpu_custom_call" | custom-call | tf_op jit(solution)/shard_map/whole_grad/pallas_call | solution.py:107
  21.7 3.6 %all-to-all-done = bf16[8,32,128]{2,1,0:T(8,128)(2,1)S(1)} async-done(((bf16[8,32,128]{2,1,0:T(8,128)(2,1)}), bf16[8,32,128]{2,1,0:T(8,128)(2,1)S(1)}, u32[]{:S(2)}, u32[]{:S(2)}) %all-to-all-start) | async-done | bytes 65568 | tf_op jit(solution)/shard_map/all_to_all | solution.py:174
  25.4 9.2 %all-to-all-start.1 = ((bf16[32,344,128]{2,1,0:T(8,128)(2,1)}), bf16[32,344,128]{2,1,0:T(8,128)(2,1)S(1)}, u32[]{:S(2)}, u32[]{:S(2)}) async-start(bf16[32,344,128]{2,1,0:T(8,128)(2,1)} %whole_grad.1), calls=%async_computation.1 | async-start | bytes 5636096 | tf_op jit(solution)/shard_map/all_to_all | solution.py:179
  34.6 43.0 %all-gather = bf16[32,32,128]{2,1,0:T(8,128)(2,1)S(1)} all-gather(bf16[8,32,128]{2,1,0:T(8,128)(2,1)S(1)} %all-to-all-done), channel_id=2, replica_groups=mesh['xl'=2,'y'=4,'core'=2,'far'=4,'near'=8,'xh'=2] {'far'}, dimensions={0}, use_global_device_ids=true | all-gather | bytes 327680 | tf_op jit(solution)/shard_map/all_gather | solution.py:177
  77.7 0.0 all-to-all-done.1.pieces
  77.7 0.0 copy-start
  77.7 0.0 copy-start.1
  77.7 1.1 partial_grad.1
  78.8 3.2 %collective-permute-start = (bf16[16,32,344]{2,1,0:T(8,128)(2,1)S(1)}, bf16[16,32,344]{2,1,0:T(8,128)(2,1)S(1)}, u32[]{:S(2)}, u32[]{:S(2)}) collective-permute-start(bf16[16,32,344]{2,1,0:T(8,128)(2,1)S(1)} %get-tuple-element.16), channel_id=1, source_target_pairs={{0,64},{64,0},{1,65},{65,1},{2,66},{66,2},{3,67},{67,3},{4,68},{68... | collective-permute-start | bytes 1056776 | tf_op jit(solution)/shard_map/ppermute | solution.py:181
  82.0 1.3 %collective-permute-done = bf16[16,32,344]{2,1,0:T(8,128)(2,1)S(1)} collective-permute-done((bf16[16,32,344]{2,1,0:T(8,128)(2,1)S(1)}, bf16[16,32,344]{2,1,0:T(8,128)(2,1)S(1)}, u32[]{:S(2)}, u32[]{:S(2)}) %collective-permute-start) | collective-permute-done | bytes 352288 | tf_op jit(solution)/shard_map/ppermute | solution.py:181
  83.3 0.1 add_convert_fusion
  83.4 15.0 %all_to_all.20 = bf16[16,32,344]{2,1,0:T(8,128)(2,1)S(1)} all-to-all(bf16[16,32,344]{2,1,0:T(8,128)(2,1)S(1)} %add_convert_fusion), channel_id=1, replica_groups=mesh['xl'=2,'y'=4,'core'=2,'far'=4,'near'=8,'xh'=2] {'xl','y','xh'}, dimensions={0} | all-to-all | bytes 704512 | tf_op jit(solution)/shard_map/all_to_all | solution.py:182
  98.4 0.1 convert_reduce_fusion
  98.5 0.0 copy-done
  98.5 0.0 copy-done.1
  98.5 0.7 divide_convert_fusion
  99.2 11.7 %all_to_all.21 = bf16[16,32,344]{2,1,0:T(8,128)(2,1)S(1)} all-to-all(bf16[16,32,344]{2,1,0:T(8,128)(2,1)S(1)} %broadcast_in_dim.2), channel_id=1, replica_groups=mesh['xl'=2,'y'=4,'core'=2,'far'=4,'near'=8,'xh'=2] {'xl','y','xh'}, dimensions={0} | all-to-all | bytes 704512 | tf_op jit(solution)/shard_map/all_to_all | solution.py:22
  110.9 5.0 %all-gather.1 = bf16[32,32,344]{2,1,0:T(8,128)(2,1)S(1)} all-gather(bf16[16,32,344]{2,1,0:T(8,128)(2,1)S(1)} %all_to_all.21), channel_id=3, replica_groups=mesh['xl'=2,'y'=4,'core'=2,'far'=4,'near'=8,'xh'=2] {'core'}, dimensions={0}, use_global_device_ids=true | all-gather | bytes 1056768 | tf_op jit(solution)/shard_map/all_gather | solution.py:189
  115.9 0.1 copy.9
  116.0 1.1 convolution_multiply_fusion
  (1 shorter events, 0.0 us)
Async XLA Ops:
  2.5 22.8 %all-to-all-start = ((bf16[8,32,128]{2,1,0:T(8,128)(2,1)}), bf16[8,32,128]{2,1,0:T(8,128)(2,1)S(1)}, u32[]{:S(2)}, u32[]{:S(2)}) async-start(bf16[8,32,128]{2,1,0:T(8,128)(2,1)} %get-tuple-element.12), calls=%async_computation | async-start | bytes 131072 | tf_op jit(solution)/shard_map/all_to_all | solution.py:174
  25.4 52.3 %all-to-all-start.1 = ((bf16[32,344,128]{2,1,0:T(8,128)(2,1)}), bf16[32,344,128]{2,1,0:T(8,128)(2,1)S(1)}, u32[]{:S(2)}, u32[]{:S(2)}) async-start(bf16[32,344,128]{2,1,0:T(8,128)(2,1)} %whole_grad.1), calls=%async_computation.1 | async-start | bytes 5636096 | tf_op jit(solution)/shard_map/all_to_all | solution.py:179
  77.7 20.8 %copy-start = (f32[32,344]{1,0:T(8,128)S(1)}, f32[32,344]{1,0:T(8,128)}, u32[]{:S(2)}) copy-start(f32[32,344]{1,0:T(8,128)} %param.9) | copy-start | bytes 132100
  77.7 20.8 %copy-start.1 = (f32[32,344]{1,0:T(8,128)S(1)}, f32[32,344]{1,0:T(8,128)}, u32[]{:S(2)}) copy-start(f32[32,344]{1,0:T(8,128)} %param.8) | copy-start | bytes 132100
  78.8 4.5 %collective-permute-start = (bf16[16,32,344]{2,1,0:T(8,128)(2,1)S(1)}, bf16[16,32,344]{2,1,0:T(8,128)(2,1)S(1)}, u32[]{:S(2)}, u32[]{:S(2)}) collective-permute-start(bf16[16,32,344]{2,1,0:T(8,128)(2,1)S(1)} %get-tuple-element.16), channel_id=1, source_target_pairs={{0,64},{64,0},{1,65},{65,1},{2,66},{66,2},{3,67},{67,3},{4,68},{68... | collective-permute-start | bytes 1056776 | tf_op jit(solution)/shard_map/ppermute | solution.py:181

commit v8 on v7

--- a/solution.py
+++ b/solution.py
@@ -198,7 +198,7 @@
 def solution(mesh):
     dp, mp, pipe = mesh.devices.shape
     fine = Mesh(
-        mesh.devices.reshape(2, dp // 4, 2, mp // 8, 8, pipe),
+        mesh.devices.reshape(2, dp // 4, 2, mp // 4, 4, pipe),
         ("xl", "y", "core", "far", "near", "xh"),
     )
     return jax.shard_map(

time: 118 us -> 113 us (0.958)
  blocking collectives: 74.8 us -> 70.7 us
  waiting for transfers between devices: 4.97 us -> 1.33 us
  starting transfers between devices: 25.5 us -> 28.5 us
    all_to_all x1, starting transfers between devices: 13.1 us -> 6.46 us  [on_device(): near_rows = lax.all_to_all(own_rows, 'near', 0, 0)]
    all_to_all x1, starting transfers between devices: 9.25 us -> 14.7 us  [on_device(): pieces = lax.all_to_all(pieces, DATA, 0, 0)]
    ppermute x1, starting transfers between devices: 3.2 us -> 7.3 us  [on_device(): sent = lax.ppermute(send, 'core', ((0, 1), (1, 0)))]
    all_gather x1, blocking collectives: 43 us -> 39 us  [on_device(): basis_rows = lax.all_gather(near_rows, 'far', axis=0).reshape(-1, rows)]
    all_to_all x1, waiting for transfers between devices: 3.64 us -> 0.01 us  [on_device(): near_rows = lax.all_to_all(own_rows, 'near', 0, 0)]
  transfers between devices with their start and end apart: 3 -> 3, of which waited for: 2 -> 1; matrix products, arithmetic and copies ran while one was open for 0% -> 0% of each run, Pallas kernels for 5% -> 5%
where the time goes in v8:
time: 113 us; the launch traced here: 112 us
  blocking collectives  70.7 us (63%)
  starting transfers between devices  28.5 us (25%)
  Pallas kernels  9.03 us (8%)
  waiting for transfers between devices  1.33 us (1%)
    all_gather x1, blocking collectives, on_device(): basis_rows = lax.all_gather(near_rows, 'far', axis=0).reshape(-1, rows)  39 us
    all_to_all x1, blocking collectives, on_device(): lax.all_to_all((keep + sent.astype(jnp.float32)).astype(jnp.bfloat16), CH...  15 us
    all_to_all x1, starting transfers between devices, on_device(): pieces = lax.all_to_all(pieces, DATA, 0, 0)  14.7 us
    all_to_all x1, blocking collectives, spread(): return lax.all_to_all(jnp.broadcast_to(x[None], (n, *x.shape)), axes, 0, 0)  11.7 us
    ppermute x1, starting transfers between devices, on_device(): sent = lax.ppermute(send, 'core', ((0, 1), (1, 0)))  7.3 us
    all_to_all x1, starting transfers between devices, on_device(): near_rows = lax.all_to_all(own_rows, 'near', 0, 0)  6.46 us
    pallas_call x1, Pallas kernels, whole_grad(): pl.pallas_call(grad_kernel, in_specs=[pl.BlockSpec(memory_space=pltpu.VME...  6.11 us
    all_gather x1, blocking collectives, on_device(): directions = lax.all_gather(spread(direction, CHIPS), 'core', axis=0)  4.96 us
  transfers between devices with their start and end apart: 3, of which 1 were waited for; matrix products, arithmetic and copies ran while one was open for 0% of the time, Pallas kernels for 5%

profile of v8, /device:TPU:1, one launch (start us, length us, event | category | flops | bytes accessed | tf_op | source)
XLA Modules:
  0.0 112.3 jit_solution(8160639204836159936)
XLA Ops:
  0.6 1.9 %stage.1 = (bf16[4,32,128]{2,1,0:T(8,128)(2,1)}, bf16[344,1024]{1,0:T(8,128)(2,1)S(1)}, bf16[1024,1024]{1,0:T(8,128)(2,1)S(1)}) custom-call(bf16[32,4096]{1,0:T(8,128)(2,1)} %bitcast.14, bf16[344,1024]{1,0:T(8,128)(2,1)} %bitcast.13, bf16[1024,4096]{1,0:T(8,128)(2,1)} %act_hbm.3), custom_call_target="tpu_custom_call" | custom-call | tf_op jit(solution)/shard_map/stage/pallas_call | solution.py:50
  2.5 6.5 %all-to-all-start = ((bf16[4,32,128]{2,1,0:T(8,128)(2,1)}), bf16[4,32,128]{2,1,0:T(8,128)(2,1)S(1)}, u32[]{:S(2)}, u32[]{:S(2)}) async-start(bf16[4,32,128]{2,1,0:T(8,128)(2,1)} %get-tuple-element.12), calls=%async_computation | async-start | bytes 65536 | tf_op jit(solution)/shard_map/all_to_all | solution.py:174
  8.9 6.1 %whole_grad.1 = bf16[32,344,128]{2,1,0:T(8,128)(2,1)} custom-call(bf16[344,1024]{1,0:T(8,128)(2,1)S(1)} %get-tuple-element.10.cot, bf16[1024,1024]{1,0:T(8,128)(2,1)S(1)} %get-tuple-element.11.first, bf16[1024,4096]{1,0:T(8,128)(2,1)} %act_hbm.3), custom_call_target="tpu_custom_call" | custom-call | tf_op jit(solution)/shard_map/whole_grad/pallas_call | solution.py:107
  15.1 0.0 all-to-all-done
  15.1 14.7 %all-to-all-start.1 = ((bf16[32,344,128]{2,1,0:T(8,128)(2,1)}), bf16[32,344,128]{2,1,0:T(8,128)(2,1)S(1)}, u32[]{:S(2)}, u32[]{:S(2)}) async-start(bf16[32,344,128]{2,1,0:T(8,128)(2,1)} %whole_grad.1), calls=%async_computation.1 | async-start | bytes 5636096 | tf_op jit(solution)/shard_map/all_to_all | solution.py:179
  29.8 39.0 %all-gather = bf16[32,32,128]{2,1,0:T(8,128)(2,1)S(1)} all-gather(bf16[4,32,128]{2,1,0:T(8,128)(2,1)S(1)} %all-to-all-done), channel_id=2, replica_groups=mesh['xl'=2,'y'=4,'core'=2,'far'=8,'near'=4,'xh'=2] {'far'}, dimensions={0}, use_global_device_ids=true | all-gather | bytes 294912 | tf_op jit(solution)/shard_map/all_gather | solution.py:177
  68.8 0.0 all-to-all-done.1.pieces
  68.8 0.0 copy-start
  68.8 0.0 copy-start.1
  68.8 1.1 partial_grad.1
  69.9 7.3 %collective-permute-start = (bf16[16,32,344]{2,1,0:T(8,128)(2,1)S(1)}, bf16[16,32,344]{2,1,0:T(8,128)(2,1)S(1)}, u32[]{:S(2)}, u32[]{:S(2)}) collective-permute-start(bf16[16,32,344]{2,1,0:T(8,128)(2,1)S(1)} %get-tuple-element.16), channel_id=1, source_target_pairs={{0,64},{64,0},{1,65},{65,1},{2,66},{66,2},{3,67},{67,3},{4,68},{68... | collective-permute-start | bytes 1056776 | tf_op jit(solution)/shard_map/ppermute | solution.py:181
  77.2 1.3 %collective-permute-done = bf16[16,32,344]{2,1,0:T(8,128)(2,1)S(1)} collective-permute-done((bf16[16,32,344]{2,1,0:T(8,128)(2,1)S(1)}, bf16[16,32,344]{2,1,0:T(8,128)(2,1)S(1)}, u32[]{:S(2)}, u32[]{:S(2)}) %collective-permute-start) | collective-permute-done | bytes 352288 | tf_op jit(solution)/shard_map/ppermute | solution.py:181
  78.6 0.1 add_convert_fusion
  78.6 15.0 %all_to_all.20 = bf16[16,32,344]{2,1,0:T(8,128)(2,1)S(1)} all-to-all(bf16[16,32,344]{2,1,0:T(8,128)(2,1)S(1)} %add_convert_fusion), channel_id=1, replica_groups=mesh['xl'=2,'y'=4,'core'=2,'far'=8,'near'=4,'xh'=2] {'xl','y','xh'}, dimensions={0} | all-to-all | bytes 704512 | tf_op jit(solution)/shard_map/all_to_all | solution.py:182
  93.6 0.1 convert_reduce_fusion
  93.7 0.0 copy-done
  93.7 0.0 copy-done.1
  93.7 0.7 divide_convert_fusion
  94.4 11.7 %all_to_all.21 = bf16[16,32,344]{2,1,0:T(8,128)(2,1)S(1)} all-to-all(bf16[16,32,344]{2,1,0:T(8,128)(2,1)S(1)} %broadcast_in_dim.2), channel_id=1, replica_groups=mesh['xl'=2,'y'=4,'core'=2,'far'=8,'near'=4,'xh'=2] {'xl','y','xh'}, dimensions={0} | all-to-all | bytes 704512 | tf_op jit(solution)/shard_map/all_to_all | solution.py:22
  106.1 5.0 %all-gather.1 = bf16[32,32,344]{2,1,0:T(8,128)(2,1)S(1)} all-gather(bf16[16,32,344]{2,1,0:T(8,128)(2,1)S(1)} %all_to_all.21), channel_id=3, replica_groups=mesh['xl'=2,'y'=4,'core'=2,'far'=8,'near'=4,'xh'=2] {'core'}, dimensions={0}, use_global_device_ids=true | all-gather | bytes 1056768 | tf_op jit(solution)/shard_map/all_gather | solution.py:189
  111.1 0.1 copy.9
  111.2 1.1 convolution_multiply_fusion
  (1 shorter events, 0.0 us)
Async XLA Ops:
  2.5 12.6 %all-to-all-start = ((bf16[4,32,128]{2,1,0:T(8,128)(2,1)}), bf16[4,32,128]{2,1,0:T(8,128)(2,1)S(1)}, u32[]{:S(2)}, u32[]{:S(2)}) async-start(bf16[4,32,128]{2,1,0:T(8,128)(2,1)} %get-tuple-element.12), calls=%async_computation | async-start | bytes 65536 | tf_op jit(solution)/shard_map/all_to_all | solution.py:174
  15.1 53.8 %all-to-all-start.1 = ((bf16[32,344,128]{2,1,0:T(8,128)(2,1)}), bf16[32,344,128]{2,1,0:T(8,128)(2,1)S(1)}, u32[]{:S(2)}, u32[]{:S(2)}) async-start(bf16[32,344,128]{2,1,0:T(8,128)(2,1)} %whole_grad.1), calls=%async_computation.1 | async-start | bytes 5636096 | tf_op jit(solution)/shard_map/all_to_all | solution.py:179
  68.8 24.8 %copy-start = (f32[32,344]{1,0:T(8,128)S(1)}, f32[32,344]{1,0:T(8,128)}, u32[]{:S(2)}) copy-start(f32[32,344]{1,0:T(8,128)} %param.9) | copy-start | bytes 132100
  68.8 24.9 %copy-start.1 = (f32[32,344]{1,0:T(8,128)S(1)}, f32[32,344]{1,0:T(8,128)}, u32[]{:S(2)}) copy-start(f32[32,344]{1,0:T(8,128)} %param.8) | copy-start | bytes 132100
  69.9 8.6 %collective-permute-start = (bf16[16,32,344]{2,1,0:T(8,128)(2,1)S(1)}, bf16[16,32,344]{2,1,0:T(8,128)(2,1)S(1)}, u32[]{:S(2)}, u32[]{:S(2)}) collective-permute-start(bf16[16,32,344]{2,1,0:T(8,128)(2,1)S(1)} %get-tuple-element.16), channel_id=1, source_target_pairs={{0,64},{64,0},{1,65},{65,1},{2,66},{66,2},{3,67},{67,3},{4,68},{68... | collective-permute-start | bytes 1056776 | tf_op jit(solution)/shard_map/ppermute | solution.py:181

commit v9 on v8

--- a/solution.py
+++ b/solution.py
@@ -174,7 +174,10 @@
     near_rows = lax.all_to_all(own_rows, "near", 0, 0)
     pieces = whole_grad(cot, first, activations, n_data)
     pieces, near_rows = lax.optimization_barrier((pieces, near_rows))
-    basis_rows = lax.all_gather(near_rows, "far", axis=0).reshape(-1, rows)
+    chip_rows = lax.all_gather(near_rows, ("far", "core"), axis=0)
+    chip_rows = chip_rows.reshape(-1, 2, *near_rows.shape)
+    basis_rows = lax.dynamic_index_in_dim(chip_rows, lax.axis_index("core"), 1, keepdims=False)
+    basis_rows = basis_rows.reshape(-1, rows)
 
     pieces = lax.all_to_all(pieces, DATA, 0, 0)
     keep, send = partial_grad(pieces, basis_rows, tile_rows)

time: 113 us -> 103 us (0.912)
  blocking collectives: 70.7 us -> 61.7 us
  starting transfers between devices: 28.5 us -> 23.7 us
  waiting for transfers between devices: 1.33 us -> 5.35 us
    all_gather x1, blocking collectives: 39 us -> 32.1 us  [on_device(): chip_rows = lax.all_gather(near_rows, ('far', 'core'), axis=0)]
    ppermute x1, starting transfers between devices: 7.3 us -> 2.53 us  [on_device(): sent = lax.ppermute(send, 'core', ((0, 1), (1, 0)))]
    all_to_all x1, waiting for transfers between devices: 0.01 us -> 4.02 us  [on_device(): pieces = lax.all_to_all(pieces, DATA, 0, 0)]
    all_to_all x1, blocking collectives: 15 us -> 13 us  [on_device(): lax.all_to_all((keep + sent.astype(jnp.float32)).astype(jnp.bfloat16), CH...]
  transfers between devices with their start and end apart: 3 -> 3, of which waited for: 1 -> 2; matrix products, arithmetic and copies ran while one was open for 0% -> 0% of each run, Pallas kernels for 5% -> 6%
where the time goes in v9:
time: 103 us
  blocking collectives  61.7 us (60%)
  starting transfers between devices  23.7 us (23%)
  Pallas kernels  9.03 us (9%)
  waiting for transfers between devices  5.35 us (5%)
  matrix products  1.1 us (1%)
    all_gather x1, blocking collectives, on_device(): chip_rows = lax.all_gather(near_rows, ('far', 'core'), axis=0)  32.1 us
    all_to_all x1, starting transfers between devices, on_device(): pieces = lax.all_to_all(pieces, DATA, 0, 0)  14.7 us
    all_to_all x1, blocking collectives, on_device(): lax.all_to_all((keep + sent.astype(jnp.float32)).astype(jnp.bfloat16), CH...  13 us
    all_to_all x1, blocking collectives, spread(): return lax.all_to_all(jnp.broadcast_to(x[None], (n, *x.shape)), axes, 0, 0)  11.7 us
    all_to_all x1, starting transfers between devices, on_device(): near_rows = lax.all_to_all(own_rows, 'near', 0, 0)  6.46 us
    pallas_call x1, Pallas kernels, whole_grad(): pl.pallas_call(grad_kernel, in_specs=[pl.BlockSpec(memory_space=pltpu.VME...  6.11 us
    all_gather x1, blocking collectives, on_device(): directions = lax.all_gather(spread(direction, CHIPS), 'core', axis=0)  4.96 us
    all_to_all x1, waiting for transfers between devices, on_device(): pieces = lax.all_to_all(pieces, DATA, 0, 0)  4.02 us
  transfers between devices with their start and end apart: 3, of which 2 were waited for; matrix products, arithmetic and copies ran while one was open for 0% of the time, Pallas kernels for 6%

profile of v9, /device:TPU:1, one launch (start us, length us, event | category | flops | bytes accessed | tf_op | source)
XLA Modules:
  0.0 102.6 jit_solution(992168187310102550)
XLA Ops:
  0.6 1.9 %stage.1 = (bf16[4,32,128]{2,1,0:T(8,128)(2,1)}, bf16[344,1024]{1,0:T(8,128)(2,1)S(1)}, bf16[1024,1024]{1,0:T(8,128)(2,1)S(1)}) custom-call(bf16[32,4096]{1,0:T(8,128)(2,1)} %bitcast.18, bf16[344,1024]{1,0:T(8,128)(2,1)} %bitcast.17, bf16[1024,4096]{1,0:T(8,128)(2,1)} %act_hbm.3), custom_call_target="tpu_custom_call" | custom-call | tf_op jit(solution)/shard_map/stage/pallas_call | solution.py:50
  2.5 6.5 %all-to-all-start = ((bf16[4,32,128]{2,1,0:T(8,128)(2,1)}), bf16[4,32,128]{2,1,0:T(8,128)(2,1)S(1)}, u32[]{:S(2)}, u32[]{:S(2)}) async-start(bf16[4,32,128]{2,1,0:T(8,128)(2,1)} %get-tuple-element.12), calls=%async_computation | async-start | bytes 65536 | tf_op jit(solution)/shard_map/all_to_all | solution.py:174
  8.9 6.1 %whole_grad.1 = bf16[32,344,128]{2,1,0:T(8,128)(2,1)} custom-call(bf16[344,1024]{1,0:T(8,128)(2,1)S(1)} %get-tuple-element.10.cot, bf16[1024,1024]{1,0:T(8,128)(2,1)S(1)} %get-tuple-element.11.first, bf16[1024,4096]{1,0:T(8,128)(2,1)} %act_hbm.3), custom_call_target="tpu_custom_call" | custom-call | tf_op jit(solution)/shard_map/whole_grad/pallas_call | solution.py:107
  15.1 0.0 all-to-all-done
  15.1 14.7 %all-to-all-start.1 = ((bf16[32,344,128]{2,1,0:T(8,128)(2,1)}), bf16[32,344,128]{2,1,0:T(8,128)(2,1)S(1)}, u32[]{:S(2)}, u32[]{:S(2)}) async-start(bf16[32,344,128]{2,1,0:T(8,128)(2,1)} %whole_grad.1), calls=%async_computation.1 | async-start | bytes 5636096 | tf_op jit(solution)/shard_map/all_to_all | solution.py:182
  29.8 32.1 %all-gather = bf16[64,32,128]{2,1,0:T(8,128)(2,1)S(1)} all-gather(bf16[4,32,128]{2,1,0:T(8,128)(2,1)S(1)} %all-to-all-done), channel_id=2, replica_groups=mesh['xl'=2,'y'=4,'core'=2,'far'=8,'near'=4,'xh'=2] {'far','core'}, dimensions={0}, use_global_device_ids=true | all-gather | bytes 557056 | tf_op jit(solution)/shard_map/all_gather | solution.py:177
  61.9 4.0 %all-to-all-done.1.pieces = bf16[32,344,128]{2,1,0:T(8,128)(2,1)S(1)} async-done(((bf16[32,344,128]{2,1,0:T(8,128)(2,1)}), bf16[32,344,128]{2,1,0:T(8,128)(2,1)S(1)}, u32[]{:S(2)}, u32[]{:S(2)}) %all-to-all-start.1) | async-done | bytes 2818080 | tf_op jit(solution)/shard_map/all_to_all | solution.py:182
  65.9 0.0 copy-start
  65.9 0.0 copy-start.1
  65.9 1.1 %partial_grad.1 = (f32[16,32,344]{2,1,0:T(8,128)S(1)}, bf16[16,32,344]{2,1,0:T(8,128)(2,1)S(1)}) custom-call(bf16[32,344,128]{2,1,0:T(8,128)(2,1)S(1)} %all-to-all-done.1.pieces, bf16[1024,128]{1,0:T(8,128)(2,1)S(1)} %bitcast.12), custom_call_target="tpu_custom_call" | custom-call | tf_op jit(solution)/shard_map/partial_grad/pallas_call | solution.py:154
  67.0 2.5 %collective-permute-start = (bf16[16,32,344]{2,1,0:T(8,128)(2,1)S(1)}, bf16[16,32,344]{2,1,0:T(8,128)(2,1)S(1)}, u32[]{:S(2)}, u32[]{:S(2)}) collective-permute-start(bf16[16,32,344]{2,1,0:T(8,128)(2,1)S(1)} %get-tuple-element.16), channel_id=1, source_target_pairs={{0,64},{64,0},{1,65},{65,1},{2,66},{66,2},{3,67},{67,3},{4,68},{68... | collective-permute-start | bytes 1056776 | tf_op jit(solution)/shard_map/ppermute | solution.py:184
  69.6 1.3 %collective-permute-done = bf16[16,32,344]{2,1,0:T(8,128)(2,1)S(1)} collective-permute-done((bf16[16,32,344]{2,1,0:T(8,128)(2,1)S(1)}, bf16[16,32,344]{2,1,0:T(8,128)(2,1)S(1)}, u32[]{:S(2)}, u32[]{:S(2)}) %collective-permute-start) | collective-permute-done | bytes 352288 | tf_op jit(solution)/shard_map/ppermute | solution.py:184
  70.9 0.1 add_convert_fusion
  71.0 13.0 %all_to_all.20 = bf16[16,32,344]{2,1,0:T(8,128)(2,1)S(1)} all-to-all(bf16[16,32,344]{2,1,0:T(8,128)(2,1)S(1)} %add_convert_fusion), channel_id=1, replica_groups=mesh['xl'=2,'y'=4,'core'=2,'far'=8,'near'=4,'xh'=2] {'xl','y','xh'}, dimensions={0} | all-to-all | bytes 704512 | tf_op jit(solution)/shard_map/all_to_all | solution.py:185
  83.9 0.1 convert_reduce_fusion
  84.0 0.0 copy-done
  84.0 0.0 copy-done.1
  84.0 0.7 divide_convert_fusion
  84.7 11.7 %all_to_all.21 = bf16[16,32,344]{2,1,0:T(8,128)(2,1)S(1)} all-to-all(bf16[16,32,344]{2,1,0:T(8,128)(2,1)S(1)} %broadcast_in_dim.2), channel_id=1, replica_groups=mesh['xl'=2,'y'=4,'core'=2,'far'=8,'near'=4,'xh'=2] {'xl','y','xh'}, dimensions={0} | all-to-all | bytes 704512 | tf_op jit(solution)/shard_map/all_to_all | solution.py:22
  96.4 5.0 %all-gather.1 = bf16[32,32,344]{2,1,0:T(8,128)(2,1)S(1)} all-gather(bf16[16,32,344]{2,1,0:T(8,128)(2,1)S(1)} %all_to_all.21), channel_id=3, replica_groups=mesh['xl'=2,'y'=4,'core'=2,'far'=8,'near'=4,'xh'=2] {'core'}, dimensions={0}, use_global_device_ids=true | all-gather | bytes 1056768 | tf_op jit(solution)/shard_map/all_gather | solution.py:192
  101.4 0.1 copy.13
  101.5 1.1 %convolution_multiply_fusion = f32[128,344]{0,1:T(8,128)} fusion(bf16[1024,128]{1,0:T(8,128)(2,1)S(1)} %bitcast.13, bf16[1024,344]{1,0:T(8,128)(2,1)S(1)} %bitcast.14), kind=kOutput, calls=%fused_computation | convolution fusion | flops 90221568 | bytes 1142784 | tf_op jit(solution)/shard_map/dot_general | solution.py:195
  (2 shorter events, 0.1 us)
Async XLA Ops:
  2.5 12.6 %all-to-all-start = ((bf16[4,32,128]{2,1,0:T(8,128)(2,1)}), bf16[4,32,128]{2,1,0:T(8,128)(2,1)S(1)}, u32[]{:S(2)}, u32[]{:S(2)}) async-start(bf16[4,32,128]{2,1,0:T(8,128)(2,1)} %get-tuple-element.12), calls=%async_computation | async-start | bytes 65536 | tf_op jit(solution)/shard_map/all_to_all | solution.py:174
  15.1 50.9 %all-to-all-start.1 = ((bf16[32,344,128]{2,1,0:T(8,128)(2,1)}), bf16[32,344,128]{2,1,0:T(8,128)(2,1)S(1)}, u32[]{:S(2)}, u32[]{:S(2)}) async-start(bf16[32,344,128]{2,1,0:T(8,128)(2,1)} %whole_grad.1), calls=%async_computation.1 | async-start | bytes 5636096 | tf_op jit(solution)/shard_map/all_to_all | solution.py:182
  65.9 18.0 %copy-start = (f32[32,344]{1,0:T(8,128)S(1)}, f32[32,344]{1,0:T(8,128)}, u32[]{:S(2)}) copy-start(f32[32,344]{1,0:T(8,128)} %param.9) | copy-start | bytes 132100
  65.9 18.1 %copy-start.1 = (f32[32,344]{1,0:T(8,128)S(1)}, f32[32,344]{1,0:T(8,128)}, u32[]{:S(2)}) copy-start(f32[32,344]{1,0:T(8,128)} %param.8) | copy-start | bytes 132100
  67.0 3.9 %collective-permute-start = (bf16[16,32,344]{2,1,0:T(8,128)(2,1)S(1)}, bf16[16,32,344]{2,1,0:T(8,128)(2,1)S(1)}, u32[]{:S(2)}, u32[]{:S(2)}) collective-permute-start(bf16[16,32,344]{2,1,0:T(8,128)(2,1)S(1)} %get-tuple-element.16), channel_id=1, source_target_pairs={{0,64},{64,0},{1,65},{65,1},{2,66},{66,2},{3,67},{67,3},{4,68},{68... | collective-permute-start | bytes 1056776 | tf_op jit(solution)/shard_map/ppermute | solution.py:184

commit v10 on v9

--- a/solution.py
+++ b/solution.py
@@ -70,14 +70,30 @@
     )(in_hbm(basis), in_hbm(cotangent), in_hbm(activations))
 
 
-def grad_kernel(cot, first, act_hbm, out_hbm, second, third, out, in_sem, out_sem):
+def grad_kernel(
+    cot, first, act_hbm, keep_hbm, send_hbm, second, third, out, in_sem, out_sem
+):
     chunks, per_chunk, width = out.shape[0], out.shape[1], out.shape[3]
-    cols = per_chunk * width
+    cols, half = per_chunk * width, per_chunk // 2
+    core = lax.axis_index("core")
+
+    def copy(c, which, to):
+        return pltpu.make_async_copy(
+            out.at[c, which * half : (which + 1) * half],
+            to.at[c * half : (c + 1) * half],
+            out_sem.at[c, which],
+        )
 
     def send(c):
-        return pltpu.make_async_copy(
-            out.at[c], out_hbm.at[c * per_chunk : (c + 1) * per_chunk], out_sem.at[c]
-        )
+        @pl.when(core == 0)
+        def _():
+            copy(c, 0, keep_hbm).start()
+            copy(c, 1, send_hbm).start()
+
+        @pl.when(core == 1)
+        def _():
+            copy(c, 0, send_hbm).start()
+            copy(c, 1, keep_hbm).start()
 
     fetches, at = {}, first.shape[1]
     for i, act in enumerate((second, third)):
@@ -95,15 +111,26 @@
             c = (at + lo) // cols
             for p in range(per_chunk):
                 out[c, p] = block[:, p * width : (p + 1) * width].astype(out.dtype)
-            send(c).start()
+            send(c)
         at += act.shape[1]
-    for c in range(chunks):
-        send(c).wait()
-
-
-def whole_grad(cotangent, first, activations, pieces, chunks=8):
+
+    @pl.when(core == 0)
+    def _():
+        for c in range(chunks):
+            copy(c, 0, keep_hbm).wait()
+            copy(c, 1, send_hbm).wait()
+
+    @pl.when(core == 1)
+    def _():
+        for c in range(chunks):
+            copy(c, 0, send_hbm).wait()
+            copy(c, 1, keep_hbm).wait()
+
+
+def whole_grad(cotangent, first, activations, pieces):
     hidden, (tokens, width) = cotangent.shape[0], activations.shape
     done, cols, dtype = first.shape[1], width // pieces, activations.dtype
+    chunks, per_chunk = pieces // 4, 4
     return pl.pallas_call(
         grad_kernel,
         in_specs=[
@@ -111,18 +138,23 @@
             pl.BlockSpec(memory_space=pltpu.VMEM),
             pl.BlockSpec(memory_space=pltpu.HBM),
         ],
-        out_specs=pl.BlockSpec(memory_space=pltpu.HBM),
-        out_shape=pltpu.HBM((pieces, hidden, cols), jnp.bfloat16),
+        out_specs=[pl.BlockSpec(memory_space=pltpu.HBM)] * 2,
+        out_shape=[pltpu.HBM((pieces // 2, hidden, cols), jnp.bfloat16)] * 2,
         scratch_shapes=[
             pltpu.VMEM((tokens, done), dtype),
             pltpu.VMEM((tokens, width - 2 * done), dtype),
-            pltpu.VMEM((chunks, pieces // chunks, hidden, cols), jnp.bfloat16),
+            pltpu.VMEM((chunks, per_chunk, hidden, cols), jnp.bfloat16),
             pltpu.SemaphoreType.DMA((2,)),
-            pltpu.SemaphoreType.DMA((chunks,)),
+            pltpu.SemaphoreType.DMA((chunks, 2)),
         ],
         compiler_params=pltpu.CompilerParams(vmem_limit_bytes=24 << 20),
         name="whole_grad",
     )(cotangent, first, in_hbm(activations))
+
+
+def with_other_core(keep, send):
+    sent = lax.ppermute(send, "core", ((0, 1), (1, 0)))
+    return (keep.astype(jnp.float32) + sent.astype(jnp.float32)).astype(jnp.bfloat16)
 
 
 def partial_kernel(pieces, basis, keep, send, partial):
@@ -149,7 +181,7 @@
 
 
 def partial_grad(pieces, basis, tile_rows):
-    tiles, hidden, ranks = pieces.shape[0] // 2, pieces.shape[1], basis.shape[0]
+    tiles, hidden, ranks = pieces.shape[0], pieces.shape[1], basis.shape[0]
     shape = (tiles, tile_rows, hidden)
     return pl.pallas_call(
         partial_kernel,
@@ -172,17 +204,18 @@
 
     own_rows, cot, first = stage(projection_basis.T, cotangent.T, activations, rows)
     near_rows = lax.all_to_all(own_rows, "near", 0, 0)
-    pieces = whole_grad(cot, first, activations, n_data)
+    keep, send = whole_grad(cot, first, activations, n_data)
+    keep, send, near_rows = lax.optimization_barrier((keep, send, near_rows))
+    pieces = with_other_core(keep, send)
     pieces, near_rows = lax.optimization_barrier((pieces, near_rows))
     chip_rows = lax.all_gather(near_rows, ("far", "core"), axis=0)
     chip_rows = chip_rows.reshape(-1, 2, *near_rows.shape)
     basis_rows = lax.dynamic_index_in_dim(chip_rows, lax.axis_index("core"), 1, keepdims=False)
     basis_rows = basis_rows.reshape(-1, rows)
 
-    pieces = lax.all_to_all(pieces, DATA, 0, 0)
+    pieces = lax.all_to_all(pieces, CHIPS, 0, 0)
     keep, send = partial_grad(pieces, basis_rows, tile_rows)
-    sent = lax.ppermute(send, "core", ((0, 1), (1, 0)))
-    tiles = lax.all_to_all((keep + sent.astype(jnp.float32)).astype(jnp.bfloat16), CHIPS, 0, 0)
+    tiles = lax.all_to_all(with_other_core(keep, send), CHIPS, 0, 0)
     grad_tile = jnp.sum(tiles.astype(jnp.float32), axis=0)
     first_new = beta_first * first_moment + (1.0 - beta_first) * grad_tile
     second_new = beta_second * second_moment + (1.0 - beta_second) * grad_tile * grad_tile

time: 103 us -> 108 us (1.049)
  other arithmetic: 0.81 us -> 3.71 us
  blocking collectives: 61.7 us -> 63.4 us
  starting transfers between devices: 23.7 us -> 25.2 us
    ppermute x1 -> x2, starting transfers between devices: 2.53 us -> 15.1 us  [with_other_core(): sent = lax.ppermute(send, 'core', ((0, 1), (1, 0)))]
    all_to_all x1, starting transfers between devices: 14.7 us -> 3.7 us  [on_device(): pieces = lax.all_to_all(pieces, CHIPS, 0, 0)]
    all_to_all x1, waiting for transfers between devices: 4.02 us -> 0.01 us  [on_device(): pieces = lax.all_to_all(pieces, CHIPS, 0, 0)]
    ppermute x1 -> x2, waiting for transfers between devices: 1.33 us -> 4.57 us  [with_other_core(): sent = lax.ppermute(send, 'core', ((0, 1), (1, 0)))]
    convert_element_type x1 -> x2, other arithmetic: 0.08 us -> 2.98 us  [with_other_core(): (keep.astype(jnp.float32) + sent.astype(jnp.float32)).astype(jnp.bfloat16)]
    all_to_all x1, blocking collectives: 13 us -> 15.4 us  [on_device(): tiles = lax.all_to_all(with_other_core(keep, send), CHIPS, 0, 0)]
  transfers between devices with their start and end apart: 3 -> 4, of which waited for: 2 -> 2; matrix products, arithmetic and copies ran while one was open for 0% -> 0% of each run, Pallas kernels for 6% -> 6%
where the time goes in v10:
time: 108 us
  blocking collectives  63.4 us (59%)
  starting transfers between devices  25.2 us (23%)
  Pallas kernels  9.02 us (8%)
  waiting for transfers between devices  4.57 us (4%)
  other arithmetic  3.71 us (3%)
  matrix products  1.1 us (1%)
    all_gather x1, blocking collectives, on_device(): chip_rows = lax.all_gather(near_rows, ('far', 'core'), axis=0)  31.7 us
    all_to_all x1, blocking collectives, on_device(): tiles = lax.all_to_all(with_other_core(keep, send), CHIPS, 0, 0)  15.4 us
    ppermute x2, starting transfers between devices, with_other_core(): sent = lax.ppermute(send, 'core', ((0, 1), (1, 0)))  15.1 us
    all_to_all x1, blocking collectives, spread(): return lax.all_to_all(jnp.broadcast_to(x[None], (n, *x.shape)), axes, 0, 0)  11.4 us
    all_to_all x1, starting transfers between devices, on_device(): near_rows = lax.all_to_all(own_rows, 'near', 0, 0)  6.46 us
    pallas_call x1, Pallas kernels, whole_grad(): pl.pallas_call(grad_kernel, in_specs=[pl.BlockSpec(memory_space=pltpu.VME...  6.28 us
    all_gather x1, blocking collectives, on_device(): directions = lax.all_gather(spread(direction, CHIPS), 'core', axis=0)  4.96 us
    ppermute x2, waiting for transfers between devices, with_other_core(): sent = lax.ppermute(send, 'core', ((0, 1), (1, 0)))  4.57 us
  transfers between devices with their start and end apart: 4, of which 2 were waited for; matrix products, arithmetic and copies ran while one was open for 0% of the time, Pallas kernels for 6%

profile of v10, /device:TPU:1, one launch (start us, length us, event | category | flops | bytes accessed | tf_op | source)
XLA Modules:
  0.0 108.0 jit_solution(12030708778663366954)
XLA Ops:
  0.6 1.9 %stage.1 = (bf16[4,32,128]{2,1,0:T(8,128)(2,1)}, bf16[344,1024]{1,0:T(8,128)(2,1)S(1)}, bf16[1024,1024]{1,0:T(8,128)(2,1)S(1)}) custom-call(bf16[32,4096]{1,0:T(8,128)(2,1)} %bitcast.18, bf16[344,1024]{1,0:T(8,128)(2,1)} %bitcast.17, bf16[1024,4096]{1,0:T(8,128)(2,1)} %act_hbm.3), custom_call_target="tpu_custom_call" | custom-call | tf_op jit(solution)/shard_map/stage/pallas_call | solution.py:50
  2.5 6.5 %all-to-all-start = ((bf16[4,32,128]{2,1,0:T(8,128)(2,1)}), bf16[4,32,128]{2,1,0:T(8,128)(2,1)S(1)}, u32[]{:S(2)}, u32[]{:S(2)}) async-start(bf16[4,32,128]{2,1,0:T(8,128)(2,1)} %get-tuple-element.19), calls=%async_computation | async-start | bytes 65536 | tf_op jit(solution)/shard_map/all_to_all | solution.py:206
  8.9 6.3 %whole_grad.1 = (bf16[16,344,128]{2,1,0:T(8,128)(2,1)}, bf16[16,344,128]{2,1,0:T(8,128)(2,1)}) custom-call(bf16[344,1024]{1,0:T(8,128)(2,1)S(1)} %get-tuple-element.15.cot, bf16[1024,1024]{1,0:T(8,128)(2,1)S(1)} %get-tuple-element.16.first, bf16[1024,4096]{1,0:T(8,128)(2,1)} %act_hbm.3), custom_call_target="tpu_custom_call" | custom-call | tf_op jit(solution)/shard_map/whole_grad/pallas_call | solution.py:134
  15.2 0.0 all-to-all-done
  15.2 12.9 %collective-permute-start = (bf16[16,344,128]{2,1,0:T(8,128)(2,1)}, bf16[16,344,128]{2,1,0:T(8,128)(2,1)S(1)}, u32[]{:S(2)}, u32[]{:S(2)}) collective-permute-start(bf16[16,344,128]{2,1,0:T(8,128)(2,1)} %get-tuple-element.21), channel_id=1, source_target_pairs={{0,64},{64,0},{1,65},{65,1},{2,66},{66,2},{3,67},{67,3},{4,68},{68... | collective-permute-start | bytes 4227080 | tf_op jit(solution)/shard_map/ppermute | solution.py:156
  28.1 3.0 %collective-permute-done = bf16[16,344,128]{2,1,0:T(8,128)(2,1)S(1)} collective-permute-done((bf16[16,344,128]{2,1,0:T(8,128)(2,1)}, bf16[16,344,128]{2,1,0:T(8,128)(2,1)S(1)}, u32[]{:S(2)}, u32[]{:S(2)}) %collective-permute-start) | collective-permute-done | bytes 1409056 | tf_op jit(solution)/shard_map/ppermute | solution.py:156
  31.1 2.9 %add_convert_fusion = bf16[16,344,128]{2,1,0:T(8,128)(2,1)} fusion(bf16[16,344,128]{2,1,0:T(8,128)(2,1)S(1)} %collective-permute-done, bf16[16,344,128]{2,1,0:T(8,128)(2,1)} %get-tuple-element.20), kind=kLoop, calls=%fused_computation | loop fusion | flops 2818048 | bytes 4227072 | tf_op jit(solution)/shard_map/convert_element_type | solution.py:157
  34.0 3.7 %all-to-all-start.1 = ((bf16[16,344,128]{2,1,0:T(8,128)(2,1)}), bf16[16,344,128]{2,1,0:T(8,128)(2,1)S(1)}, u32[]{:S(2)}, u32[]{:S(2)}) async-start(bf16[16,344,128]{2,1,0:T(8,128)(2,1)} %add_convert_fusion), calls=%async_computation.1 | async-start | bytes 2818048 | tf_op jit(solution)/shard_map/all_to_all | solution.py:216
  37.7 31.7 %all-gather = bf16[64,32,128]{2,1,0:T(8,128)(2,1)S(1)} all-gather(bf16[4,32,128]{2,1,0:T(8,128)(2,1)S(1)} %all-to-all-done), channel_id=2, replica_groups=mesh['xl'=2,'y'=4,'core'=2,'far'=8,'near'=4,'xh'=2] {'far','core'}, dimensions={0}, use_global_device_ids=true | all-gather | bytes 557056 | tf_op jit(solution)/shard_map/all_gather | solution.py:211
  69.5 0.0 all-to-all-done.1.pieces
  69.5 0.9 partial_grad.1
  70.4 0.0 copy-start
  70.4 0.0 copy-start.1
  70.4 2.2 %collective-permute-start.1 = (bf16[16,32,344]{2,1,0:T(8,128)(2,1)S(1)}, bf16[16,32,344]{2,1,0:T(8,128)(2,1)S(1)}, u32[]{:S(2)}, u32[]{:S(2)}) collective-permute-start(bf16[16,32,344]{2,1,0:T(8,128)(2,1)S(1)} %get-tuple-element.26), channel_id=1, source_target_pairs={{0,64},{64,0},{1,65},{65,1},{2,66},{66,2},{3,67},{67,3},{4,68},{68... | collective-permute-start | bytes 1056776 | tf_op jit(solution)/shard_map/ppermute | solution.py:156
  72.6 1.6 %collective-permute-done.1 = bf16[16,32,344]{2,1,0:T(8,128)(2,1)S(1)} collective-permute-done((bf16[16,32,344]{2,1,0:T(8,128)(2,1)S(1)}, bf16[16,32,344]{2,1,0:T(8,128)(2,1)S(1)}, u32[]{:S(2)}, u32[]{:S(2)}) %collective-permute-start.1) | collective-permute-done | bytes 352288 | tf_op jit(solution)/shard_map/ppermute | solution.py:156
  74.2 0.1 add_convert_fusion.1
  74.3 15.4 %all_to_all.20 = bf16[16,32,344]{2,1,0:T(8,128)(2,1)S(1)} all-to-all(bf16[16,32,344]{2,1,0:T(8,128)(2,1)S(1)} %add_convert_fusion.1), channel_id=1, replica_groups=mesh['xl'=2,'y'=4,'core'=2,'far'=8,'near'=4,'xh'=2] {'xl','y','xh'}, dimensions={0} | all-to-all | bytes 704512 | tf_op jit(solution)/shard_map/all_to_all | solution.py:218
  89.6 0.1 convert_reduce_fusion
  89.7 0.0 copy-done
  89.7 0.0 copy-done.1
  89.7 0.7 divide_convert_fusion
  90.4 11.4 %all_to_all.21 = bf16[16,32,344]{2,1,0:T(8,128)(2,1)S(1)} all-to-all(bf16[16,32,344]{2,1,0:T(8,128)(2,1)S(1)} %broadcast_in_dim.2), channel_id=1, replica_groups=mesh['xl'=2,'y'=4,'core'=2,'far'=8,'near'=4,'xh'=2] {'xl','y','xh'}, dimensions={0} | all-to-all | bytes 704512 | tf_op jit(solution)/shard_map/all_to_all | solution.py:22
  101.8 5.0 %all-gather.1 = bf16[32,32,344]{2,1,0:T(8,128)(2,1)S(1)} all-gather(bf16[16,32,344]{2,1,0:T(8,128)(2,1)S(1)} %all_to_all.21), channel_id=3, replica_groups=mesh['xl'=2,'y'=4,'core'=2,'far'=8,'near'=4,'xh'=2] {'core'}, dimensions={0}, use_global_device_ids=true | all-gather | bytes 1056768 | tf_op jit(solution)/shard_map/all_gather | solution.py:225
  106.8 0.1 copy.13
  106.9 1.1 %convolution_multiply_fusion = f32[128,344]{0,1:T(8,128)} fusion(bf16[1024,128]{1,0:T(8,128)(2,1)S(1)} %bitcast.13, bf16[1024,344]{1,0:T(8,128)(2,1)S(1)} %bitcast.14), kind=kOutput, calls=%fused_computation.1 | convolution fusion | flops 90221568 | bytes 1142784 | tf_op jit(solution)/shard_map/dot_general | solution.py:228
  (2 shorter events, 0.1 us)
Async XLA Ops:
  2.5 12.7 %all-to-all-start = ((bf16[4,32,128]{2,1,0:T(8,128)(2,1)}), bf16[4,32,128]{2,1,0:T(8,128)(2,1)S(1)}, u32[]{:S(2)}, u32[]{:S(2)}) async-start(bf16[4,32,128]{2,1,0:T(8,128)(2,1)} %get-tuple-element.19), calls=%async_computation | async-start | bytes 65536 | tf_op jit(solution)/shard_map/all_to_all | solution.py:206
  15.2 15.9 %collective-permute-start = (bf16[16,344,128]{2,1,0:T(8,128)(2,1)}, bf16[16,344,128]{2,1,0:T(8,128)(2,1)S(1)}, u32[]{:S(2)}, u32[]{:S(2)}) collective-permute-start(bf16[16,344,128]{2,1,0:T(8,128)(2,1)} %get-tuple-element.21), channel_id=1, source_target_pairs={{0,64},{64,0},{1,65},{65,1},{2,66},{66,2},{3,67},{67,3},{4,68},{68... | collective-permute-start | bytes 4227080 | tf_op jit(solution)/shard_map/ppermute | solution.py:156
  34.0 35.5 %all-to-all-start.1 = ((bf16[16,344,128]{2,1,0:T(8,128)(2,1)}), bf16[16,344,128]{2,1,0:T(8,128)(2,1)S(1)}, u32[]{:S(2)}, u32[]{:S(2)}) async-start(bf16[16,344,128]{2,1,0:T(8,128)(2,1)} %add_convert_fusion), calls=%async_computation.1 | async-start | bytes 2818048 | tf_op jit(solution)/shard_map/all_to_all | solution.py:216
  70.4 19.3 %copy-start = (f32[32,344]{1,0:T(8,128)S(1)}, f32[32,344]{1,0:T(8,128)}, u32[]{:S(2)}) copy-start(f32[32,344]{1,0:T(8,128)} %param.9) | copy-start | bytes 132100
  70.4 19.3 %copy-start.1 = (f32[32,344]{1,0:T(8,128)S(1)}, f32[32,344]{1,0:T(8,128)}, u32[]{:S(2)}) copy-start(f32[32,344]{1,0:T(8,128)} %param.8) | copy-start | bytes 132100
  70.4 3.7 %collective-permute-start.1 = (bf16[16,32,344]{2,1,0:T(8,128)(2,1)S(1)}, bf16[16,32,344]{2,1,0:T(8,128)(2,1)S(1)}, u32[]{:S(2)}, u32[]{:S(2)}) collective-permute-start(bf16[16,32,344]{2,1,0:T(8,128)(2,1)S(1)} %get-tuple-element.26), channel_id=1, source_target_pairs={{0,64},{64,0},{1,65},{65,1},{2,66},{66,2},{3,67},{67,3},{4,68},{68... | collective-permute-start | bytes 1056776 | tf_op jit(solution)/shard_map/ppermute | solution.py:156

commit v11 on v9

--- a/solution.py
+++ b/solution.py
@@ -201,7 +201,7 @@
 def solution(mesh):
     dp, mp, pipe = mesh.devices.shape
     fine = Mesh(
-        mesh.devices.reshape(2, dp // 4, 2, mp // 4, 4, pipe),
+        mesh.devices.reshape(2, dp // 4, 2, mp // 2, 2, pipe),
         ("xl", "y", "core", "far", "near", "xh"),
     )
     return jax.shard_map(

time: 103 us -> 109 us (1.058)
  blocking collectives: 61.7 us -> 71.7 us
  waiting for transfers between devices: 5.35 us -> 1.6 us
    all_gather x1, blocking collectives: 32.1 us -> 39.8 us  [on_device(): chip_rows = lax.all_gather(near_rows, ('far', 'core'), axis=0)]
    all_to_all x1, waiting for transfers between devices: 4.02 us -> 0.01 us  [on_device(): pieces = lax.all_to_all(pieces, DATA, 0, 0)]
    all_to_all x1, starting transfers between devices: 6.46 us -> 3.75 us  [on_device(): near_rows = lax.all_to_all(own_rows, 'near', 0, 0)]
    all_to_all x1, starting transfers between devices: 14.7 us -> 17.4 us  [on_device(): pieces = lax.all_to_all(pieces, DATA, 0, 0)]
    all_to_all x1, blocking collectives: 13 us -> 15.6 us  [on_device(): lax.all_to_all((keep + sent.astype(jnp.float32)).astype(jnp.bfloat16), CH...]
  transfers between devices with their start and end apart: 3 -> 3, of which waited for: 2 -> 1; matrix products, arithmetic and copies ran while one was open for 0% -> 0% of each run, Pallas kernels for 6% -> 6%
where the time goes in v11:
time: 109 us; the launch traced here: 108 us
  blocking collectives  71.7 us (66%)
  starting transfers between devices  23.2 us (21%)
  Pallas kernels  9.01 us (8%)
  waiting for transfers between devices  1.6 us (1%)
  matrix products  1.1 us (1%)
    all_gather x1, blocking collectives, on_device(): chip_rows = lax.all_gather(near_rows, ('far', 'core'), axis=0)  39.8 us
    all_to_all x1, starting transfers between devices, on_device(): pieces = lax.all_to_all(pieces, DATA, 0, 0)  17.4 us
    all_to_all x1, blocking collectives, on_device(): lax.all_to_all((keep + sent.astype(jnp.float32)).astype(jnp.bfloat16), CH...  15.6 us
    all_to_all x1, blocking collectives, spread(): return lax.all_to_all(jnp.broadcast_to(x[None], (n, *x.shape)), axes, 0, 0)  11.4 us
    pallas_call x1, Pallas kernels, whole_grad(): pl.pallas_call(grad_kernel, in_specs=[pl.BlockSpec(memory_space=pltpu.VME...  6.11 us
    all_gather x1, blocking collectives, on_device(): directions = lax.all_gather(spread(direction, CHIPS), 'core', axis=0)  4.96 us
    all_to_all x1, starting transfers between devices, on_device(): near_rows = lax.all_to_all(own_rows, 'near', 0, 0)  3.75 us
  transfers between devices with their start and end apart: 3, of which 1 were waited for; matrix products, arithmetic and copies ran while one was open for 0% of the time, Pallas kernels for 6%

profile of v11, /device:TPU:1, one launch (start us, length us, event | category | flops | bytes accessed | tf_op | source)
XLA Modules:
  0.0 108.3 jit_solution(15423516996203707886)
XLA Ops:
  0.6 1.8 %stage.1 = (bf16[2,32,128]{2,1,0:T(8,128)(2,1)}, bf16[344,1024]{1,0:T(8,128)(2,1)S(1)}, bf16[1024,1024]{1,0:T(8,128)(2,1)S(1)}) custom-call(bf16[32,4096]{1,0:T(8,128)(2,1)} %bitcast.18, bf16[344,1024]{1,0:T(8,128)(2,1)} %bitcast.17, bf16[1024,4096]{1,0:T(8,128)(2,1)} %act_hbm.3), custom_call_target="tpu_custom_call" | custom-call | tf_op jit(solution)/shard_map/stage/pallas_call | solution.py:50
  2.5 3.7 %all-to-all-start = ((bf16[2,32,128]{2,1,0:T(8,128)(2,1)}), bf16[2,32,128]{2,1,0:T(8,128)(2,1)S(1)}, u32[]{:S(2)}, u32[]{:S(2)}) async-start(bf16[2,32,128]{2,1,0:T(8,128)(2,1)} %get-tuple-element.12), calls=%async_computation | async-start | bytes 32768 | tf_op jit(solution)/shard_map/all_to_all | solution.py:174
  6.2 6.1 %whole_grad.1 = bf16[32,344,128]{2,1,0:T(8,128)(2,1)} custom-call(bf16[344,1024]{1,0:T(8,128)(2,1)S(1)} %get-tuple-element.10.cot, bf16[1024,1024]{1,0:T(8,128)(2,1)S(1)} %get-tuple-element.11.first, bf16[1024,4096]{1,0:T(8,128)(2,1)} %act_hbm.3), custom_call_target="tpu_custom_call" | custom-call | tf_op jit(solution)/shard_map/whole_grad/pallas_call | solution.py:107
  12.3 0.0 all-to-all-done
  12.3 17.4 %all-to-all-start.1 = ((bf16[32,344,128]{2,1,0:T(8,128)(2,1)}), bf16[32,344,128]{2,1,0:T(8,128)(2,1)S(1)}, u32[]{:S(2)}, u32[]{:S(2)}) async-start(bf16[32,344,128]{2,1,0:T(8,128)(2,1)} %whole_grad.1), calls=%async_computation.1 | async-start | bytes 5636096 | tf_op jit(solution)/shard_map/all_to_all | solution.py:182
  29.8 39.8 %all-gather = bf16[64,32,128]{2,1,0:T(8,128)(2,1)S(1)} all-gather(bf16[2,32,128]{2,1,0:T(8,128)(2,1)S(1)} %all-to-all-done), channel_id=2, replica_groups=mesh['xl'=2,'y'=4,'core'=2,'far'=16,'near'=2,'xh'=2] {'far','core'}, dimensions={0}, use_global_device_ids=true | all-gather | bytes 540672 | tf_op jit(solution)/shard_map/all_gather | solution.py:177
  69.6 0.0 all-to-all-done.1.pieces
  69.6 0.0 copy-start
  69.6 0.0 copy-start.1
  69.6 1.1 partial_grad.1
  70.7 2.0 %collective-permute-start = (bf16[16,32,344]{2,1,0:T(8,128)(2,1)S(1)}, bf16[16,32,344]{2,1,0:T(8,128)(2,1)S(1)}, u32[]{:S(2)}, u32[]{:S(2)}) collective-permute-start(bf16[16,32,344]{2,1,0:T(8,128)(2,1)S(1)} %get-tuple-element.16), channel_id=1, source_target_pairs={{0,64},{64,0},{1,65},{65,1},{2,66},{66,2},{3,67},{67,3},{4,68},{68... | collective-permute-start | bytes 1056776 | tf_op jit(solution)/shard_map/ppermute | solution.py:184
  72.7 1.6 %collective-permute-done = bf16[16,32,344]{2,1,0:T(8,128)(2,1)S(1)} collective-permute-done((bf16[16,32,344]{2,1,0:T(8,128)(2,1)S(1)}, bf16[16,32,344]{2,1,0:T(8,128)(2,1)S(1)}, u32[]{:S(2)}, u32[]{:S(2)}) %collective-permute-start) | collective-permute-done | bytes 352288 | tf_op jit(solution)/shard_map/ppermute | solution.py:184
  74.3 0.1 add_convert_fusion
  74.4 15.6 %all_to_all.20 = bf16[16,32,344]{2,1,0:T(8,128)(2,1)S(1)} all-to-all(bf16[16,32,344]{2,1,0:T(8,128)(2,1)S(1)} %add_convert_fusion), channel_id=1, replica_groups=mesh['xl'=2,'y'=4,'core'=2,'far'=16,'near'=2,'xh'=2] {'xl','y','xh'}, dimensions={0} | all-to-all | bytes 704512 | tf_op jit(solution)/shard_map/all_to_all | solution.py:185
  89.9 0.1 convert_reduce_fusion
  90.0 0.0 copy-done
  90.0 0.0 copy-done.1
  90.0 0.7 divide_convert_fusion
  90.7 11.4 %all_to_all.21 = bf16[16,32,344]{2,1,0:T(8,128)(2,1)S(1)} all-to-all(bf16[16,32,344]{2,1,0:T(8,128)(2,1)S(1)} %broadcast_in_dim.2), channel_id=1, replica_groups=mesh['xl'=2,'y'=4,'core'=2,'far'=16,'near'=2,'xh'=2] {'xl','y','xh'}, dimensions={0} | all-to-all | bytes 704512 | tf_op jit(solution)/shard_map/all_to_all | solution.py:22
  102.1 5.0 %all-gather.1 = bf16[32,32,344]{2,1,0:T(8,128)(2,1)S(1)} all-gather(bf16[16,32,344]{2,1,0:T(8,128)(2,1)S(1)} %all_to_all.21), channel_id=3, replica_groups=mesh['xl'=2,'y'=4,'core'=2,'far'=16,'near'=2,'xh'=2] {'core'}, dimensions={0}, use_global_device_ids=true | all-gather | bytes 1056768 | tf_op jit(solution)/shard_map/all_gather | solution.py:192
  107.1 0.1 copy.13
  107.2 1.1 %convolution_multiply_fusion = f32[128,344]{0,1:T(8,128)} fusion(bf16[1024,128]{1,0:T(8,128)(2,1)S(1)} %bitcast.13, bf16[1024,344]{1,0:T(8,128)(2,1)S(1)} %bitcast.14), kind=kOutput, calls=%fused_computation | convolution fusion | flops 90221568 | bytes 1142784 | tf_op jit(solution)/shard_map/dot_general | solution.py:195
  (2 shorter events, 0.1 us)
Async XLA Ops:
  2.5 9.9 %all-to-all-start = ((bf16[2,32,128]{2,1,0:T(8,128)(2,1)}), bf16[2,32,128]{2,1,0:T(8,128)(2,1)S(1)}, u32[]{:S(2)}, u32[]{:S(2)}) async-start(bf16[2,32,128]{2,1,0:T(8,128)(2,1)} %get-tuple-element.12), calls=%async_computation | async-start | bytes 32768 | tf_op jit(solution)/shard_map/all_to_all | solution.py:174
  12.3 57.2 %all-to-all-start.1 = ((bf16[32,344,128]{2,1,0:T(8,128)(2,1)}), bf16[32,344,128]{2,1,0:T(8,128)(2,1)S(1)}, u32[]{:S(2)}, u32[]{:S(2)}) async-start(bf16[32,344,128]{2,1,0:T(8,128)(2,1)} %whole_grad.1), calls=%async_computation.1 | async-start | bytes 5636096 | tf_op jit(solution)/shard_map/all_to_all | solution.py:182
  69.6 20.5 %copy-start = (f32[32,344]{1,0:T(8,128)S(1)}, f32[32,344]{1,0:T(8,128)}, u32[]{:S(2)}) copy-start(f32[32,344]{1,0:T(8,128)} %param.9) | copy-start | bytes 132100
  69.6 20.4 %copy-start.1 = (f32[32,344]{1,0:T(8,128)S(1)}, f32[32,344]{1,0:T(8,128)}, u32[]{:S(2)}) copy-start(f32[32,344]{1,0:T(8,128)} %param.8) | copy-start | bytes 132100
  70.7 3.6 %collective-permute-start = (bf16[16,32,344]{2,1,0:T(8,128)(2,1)S(1)}, bf16[16,32,344]{2,1,0:T(8,128)(2,1)S(1)}, u32[]{:S(2)}, u32[]{:S(2)}) collective-permute-start(bf16[16,32,344]{2,1,0:T(8,128)(2,1)S(1)} %get-tuple-element.16), channel_id=1, source_target_pairs={{0,64},{64,0},{1,65},{65,1},{2,66},{66,2},{3,67},{67,3},{4,68},{68... | collective-permute-start | bytes 1056776 | tf_op jit(solution)/shard_map/ppermute | solution.py:184
